TPU v7x, 128 devices: a whole 4x4x4 slice. The times are simulated.
128 devices in a mesh: gx: 8 (over x, core), gy: 16 (over z, y).
Axes of the slice: x: 4, y: 4, z: 4, core: 2. Of those that a mesh axis runs over, the one named last changes fastest.
Arguments:
- latent: bfloat16 [128, 256, 1024], P('gx', 'gy'), may hold values from -6 to 6
- conv_first: bfloat16 [64, 1728], replicated, may hold values from -0.15625 to 0.15625
- conv_second: bfloat16 [64, 1728], replicated, may hold values from -0.15625 to 0.15625
- w_in: bfloat16 [320, 256], replicated, may hold values from -0.3125 to 0.3125
- w_out: bfloat16 [4, 256], replicated, may hold values from -0.375 to 0.375
- touch: int32 [128, 128], P(('gx', 'gy')), may hold values from -1 to 63, as said below
- anchor: int32 [524288], P(('gx', 'gy')), may hold values from 21 to 8170, as said below
- frac: float32 [3, 524288], P(None, ('gx', 'gy')), may hold values from -0.5 to 0.5
- pfeat: bfloat16 [256, 524288], P(None, ('gx', 'gy')), may hold values from -6 to 6
- cotangent: float32 [4, 524288], P(None, ('gx', 'gy')), may hold values from -48 to 48
Outputs:
- predicted: float32 [4, 524288], P(None, ('gx', 'gy'))
- feature_grads: bfloat16 [256, 524288], P(None, ('gx', 'gy'))
- grid_grad: float32 [128, 256, 1024], P('gx', 'gy')
Inputs may be any that keep to these rules, and one draw needn't show every extreme that they name: Row d is device d's touch list: entries o * 1 to o + 1 - 1 name local tiles of owner device o, or -1 for an unused slot; within each such block used slots come first. In every draw some owner is named in all 1 slots of every row, and some other owner in none. For particle p of device d = p // 4096: anchor[p] = s * 4**3 + (ix * 4 + iy) * 4 + iz, where s is a used slot of row d of touch and ix, iy, iz lie in 1 to 2. Every used slot of row d is the slot of some particle of device d.
All inputs are finite; a program needn't handle non-finite values.
Results may differ from a plain program's by a relative error of at most 0.0051.
Values may be sent and summed in bfloat16 or wider, within the bound.
A program may use at most 192 MiB of HBM per device.

v0:
```python
import jax
import jax.numpy as jnp
from jax import lax
from jax.sharding import PartitionSpec as P

TS = 4
CAP = 1


def with_halo(block, sides, width):
    for axis, dim in sides:
        count = lax.axis_size(axis)
        forward = [(i, i + 1) for i in range(count - 1)]
        backward = [(target, source) for source, target in forward]
        low = lax.ppermute(
            lax.slice_in_dim(block, block.shape[dim] - width, None, axis=dim), axis, forward
        )
        high = lax.ppermute(lax.slice_in_dim(block, 0, width, axis=dim), axis, backward)
        block = jnp.concatenate([low, block, high], axis=dim)
    return block


def conv_core(padded, weight, rows_x, rows_y, depth_cells, channels):
    cube = padded.reshape(rows_x + 2, rows_y + 2, depth_cells, channels)
    cube = jnp.pad(cube, ((0, 0), (0, 0), (1, 1), (0, 0)))
    pieces = []
    for shift_x in range(3):
        for shift_y in range(3):
            for shift_z in range(3):
                pieces.append(
                    cube[
                        shift_x : shift_x + rows_x,
                        shift_y : shift_y + rows_y,
                        shift_z : shift_z + depth_cells,
                        :,
                    ]
                )
    stacked = jnp.concatenate(pieces, axis=-1).reshape(-1, 27 * channels)
    summed = lax.dot_general(
        stacked, weight, (((1,), (1,)), ((), ())), preferred_element_type=jnp.float32
    )
    return summed.reshape(rows_x, rows_y, depth_cells * channels)


def to_tiles(field, rows_x, rows_y, depth_cells, channels):
    cube = field.reshape(rows_x // TS, TS, rows_y // TS, TS, depth_cells // TS, TS, channels)
    return cube.transpose(0, 2, 4, 1, 3, 5, 6).reshape(-1, TS**3 * channels)


def from_tiles(tiles, rows_x, rows_y, depth_cells, channels):
    cube = tiles.reshape(rows_x // TS, rows_y // TS, depth_cells // TS, TS, TS, TS, channels)
    return cube.transpose(0, 3, 1, 4, 2, 5, 6).reshape(rows_x, rows_y, depth_cells * channels)


def decode(cell_rows, anchor, frac, features, cotangent, w_in, w_out):
    particle_count = anchor.shape[0]
    block_rows = min(2048, particle_count)
    block_count = particle_count // block_rows
    channels = cell_rows.shape[1]
    neighbor = jnp.arange(27, dtype=jnp.int32)
    step_x = neighbor // 9 - 1
    step_y = neighbor // 3 % 3 - 1
    step_z = neighbor % 3 - 1
    cell_shift = step_x * (TS * TS) + step_y * TS + step_z
    unit_x = step_x.astype(jnp.float32)
    unit_y = step_y.astype(jnp.float32)
    unit_z = step_z.astype(jnp.float32)
    w_sample = w_in[:channels]
    w_state = w_in[channels:]
    w_back = w_out.astype(jnp.float32)

    def advance(block_index, running):
        partial_value, predicted, feature_grads = running
        first_row = block_index * block_rows
        anchor_rows = lax.dynamic_slice_in_dim(anchor, first_row, block_rows, 0)
        offsets = lax.dynamic_slice_in_dim(frac, first_row, block_rows, 1)
        state_rows = lax.dynamic_slice_in_dim(features, first_row, block_rows, 1)
        cot_rows = lax.dynamic_slice_in_dim(cotangent, first_row, block_rows, 1)
        distance = (
            (offsets[0][:, None] - unit_x[None, :]) ** 2
            + (offsets[1][:, None] - unit_y[None, :]) ** 2
            + (offsets[2][:, None] - unit_z[None, :]) ** 2
        )
        kernel = jnp.exp(-distance)
        weights = kernel / jnp.sum(kernel, axis=1, keepdims=True)
        targets = anchor_rows[:, None] + cell_shift[None, :]
        picked = jnp.take(cell_rows, targets, axis=0)
        sampled = jnp.sum(weights[:, :, None] * picked.astype(jnp.float32), axis=1).astype(
            jnp.bfloat16
        )
        preact = jnp.dot(sampled, w_sample, preferred_element_type=jnp.float32) + lax.dot_general(
            state_rows, w_state, (((0,), (0,)), ((), ())), preferred_element_type=jnp.float32
        )
        active, gelu_back = jax.vjp(jax.nn.gelu, preact)
        active = active.astype(jnp.bfloat16)
        pred_rows = lax.dot_general(
            w_out, active, (((1,), (1,)), ((), ())), preferred_element_type=jnp.float32
        )
        grad_active = lax.dot_general(
            cot_rows,
            w_back,
            (((0,), (0,)), ((), ())),
            precision=lax.Precision.HIGHEST,
            preferred_element_type=jnp.float32,
        )
        grad_preact = gelu_back(grad_active)[0].astype(jnp.bfloat16)
        grad_state = lax.dot_general(
            w_state, grad_preact, (((1,), (1,)), ((), ())), preferred_element_type=jnp.float32
        ).astype(jnp.bfloat16)
        grad_sampled = lax.dot_general(
            grad_preact, w_sample, (((1,), (1,)), ((), ())), preferred_element_type=jnp.float32
        )
        spread = weights[:, :, None] * grad_sampled[:, None, :]
        partial_value = partial_value.at[targets.reshape(-1)].add(spread.reshape(-1, channels))
        predicted = lax.dynamic_update_slice_in_dim(predicted, pred_rows, first_row, 1)
        feature_grads = lax.dynamic_update_slice_in_dim(feature_grads, grad_state, first_row, 1)
        return (partial_value, predicted, feature_grads)

    initial = (
        jnp.zeros(cell_rows.shape, jnp.float32),
        jnp.zeros((w_out.shape[0], particle_count), jnp.float32),
        jnp.zeros((features.shape[0], particle_count), jnp.bfloat16),
    )
    partial_value, predicted, feature_grads = lax.fori_loop(0, block_count, advance, initial)
    return (predicted, feature_grads, partial_value.astype(jnp.bfloat16))


def route_requests(wanted):
    return lax.all_to_all(wanted, ("gx", "gy"), split_axis=0, concat_axis=0, tiled=True)


def route_tiles(outgoing):
    return lax.all_to_all(outgoing, ("gx", "gy"), split_axis=0, concat_axis=0, tiled=True)


def route_grads(partial_blocks):
    return lax.all_to_all(partial_blocks, ("gx", "gy"), split_axis=0, concat_axis=0, tiled=True)


def body(latent, conv_first, conv_second, w_in, w_out, touch, anchor, frac, pfeat, cotangent):
    rows_x, rows_y, row_width = latent.shape
    channels = conv_first.shape[0]
    depth_cells = row_width // channels

    def convolve(field, weight):
        padded = with_halo(field, (("gx", 0), ("gy", 1)), 1)
        return conv_core(padded, weight, rows_x, rows_y, depth_cells, channels)

    hidden_field = jax.nn.gelu(convolve(latent, conv_first)).astype(jnp.bfloat16)
    grid_field = (latent.astype(jnp.float32) + convolve(hidden_field, conv_second)).astype(
        jnp.bfloat16
    )
    tile_rows = to_tiles(grid_field, rows_x, rows_y, depth_cells, channels)
    wanted = touch.reshape(-1, CAP)
    requested = route_requests(wanted)
    present = requested >= 0
    outgoing = jnp.where(
        present[:, :, None],
        jnp.take(tile_rows, jnp.maximum(requested, 0), axis=0),
        jnp.zeros((), jnp.bfloat16),
    )
    received = route_tiles(outgoing)
    predicted, feature_grads, partial_value = decode(
        received.reshape(-1, channels), anchor, frac, pfeat, cotangent, w_in, w_out
    )
    returned = route_grads(partial_value.reshape(received.shape))
    selector = (
        jnp.arange(tile_rows.shape[0], dtype=jnp.int32)[:, None] == requested.reshape(1, -1)
    ).astype(jnp.bfloat16)
    grad_tiles = jnp.dot(
        selector, returned.reshape(-1, returned.shape[2]), preferred_element_type=jnp.float32
    )
    grid_grad = from_tiles(grad_tiles, rows_x, rows_y, depth_cells, channels)
    return (predicted, feature_grads, grid_grad)


def solution(mesh):
    placed = (
        P("gx", "gy", None),
        P(),
        P(),
        P(),
        P(),
        P(("gx", "gy"), None),
        P(("gx", "gy")),
        P(None, ("gx", "gy")),
        P(None, ("gx", "gy")),
        P(None, ("gx", "gy")),
    )
    return jax.shard_map(
        body,
        mesh=mesh,
        in_specs=placed,
        out_specs=(P(None, ("gx", "gy")), P(None, ("gx", "gy")), P("gx", "gy", None)),
        check_vma=False,
    )
```

profile of v0, /device:TPU:0, one launch (start us, length us, event | category | flops | bytes accessed | tf_op | source)
XLA Modules:
  0.0 1542.6 jit_solution(353565947499152046)
XLA Ops:
  4.1 12.7 all-to-all-start
  20.1 2.9 collective-permute-start.2
  26.3 4.6 compare_reduce_fusion.1
  32.3 3.3 fusion.54
  35.6 8.9 pad_slice_fusion.18
  44.5 30.9 %concatenate.20 = bf16[16,16,16,1728]{3,2,1,0:T(8,128)(2,1)} concatenate(bf16[16,16,16,64]{3,2,1,0:T(8,128)(2,1)} %get-tuple-element.599, bf16[16,16,16,64]{3,2,1,0:T(8,128)(2,1)} %get-tuple-element.598, bf16[16,16,16,64]{3,2,1,0:T(8,128)(2,1)} %get-tuple-element.574, bf16[16,16,16,64]{3,2,1,0:T(8,128)(2,1)} %get-tuple-element.575, bf16[16,16,16,64]{3,2,1,0:T(8,128)(2,1)} %get-tuple-element.597, ...), dimensions={3} | concatenate | bytes 28311552 | tf_op jit(solution)/shard_map/concatenate | solution.py:38
  75.4 7.2 fusion.60
  85.8 12.0 collective-permute-start.5
  97.8 5.1 fusion.52
  103.0 4.3 collective-permute-start.6
  109.8 4.4 collective-permute-done.7
  115.6 3.3 fusion.53
  118.9 8.9 pad_slice_fusion
  127.8 31.0 %concatenate.23 = bf16[16,16,16,1728]{3,2,1,0:T(8,128)(2,1)} concatenate(bf16[16,16,16,64]{3,2,1,0:T(8,128)(2,1)} %get-tuple-element.572, bf16[16,16,16,64]{3,2,1,0:T(8,128)(2,1)} %get-tuple-element.571, bf16[16,16,16,64]{3,2,1,0:T(8,128)(2,1)} %get-tuple-element.547, bf16[16,16,16,64]{3,2,1,0:T(8,128)(2,1)} %get-tuple-element.548, bf16[16,16,16,64]{3,2,1,0:T(8,128)(2,1)} %get-tuple-element.570, ...), dimensions={3} | concatenate | bytes 28311552 | tf_op jit(solution)/shard_map/concatenate | solution.py:38
  158.7 7.2 fusion.61
  174.6 14.4 all-to-all-start.1
  190.3 17.7 %all-to-all-done.1 = bf16[128,2,2048]{2,1,0:T(2,128)(2,1)S(1)} async-done(((bf16[128,2,2048]{2,1,0:T(2,128)(2,1)}), bf16[128,2,2048]{2,1,0:T(2,128)(2,1)S(1)}, u32[]{:S(2)}, u32[]{:S(2)}) %all-to-all-start.1) | async-done | bytes 1048608 | tf_op jit(solution)/shard_map/all_to_all | solution.py:133
  209.1 6.4 reduce.3
  215.5 2.3 reshape.454
  220.0 2.3 broadcast_in_dim.91
  222.2 1272.5 %while.21 = (s32[]{:T(128)}, f32[8192,64]{1,0:T(8,128)}, f32[4,4096]{1,0:T(4,128)}, bf16[256,4096]{1,0:T(8,128)(2,1)}, s32[4096]{0:T(1024)}, /*index=5*/f32[3,40...) while((s32[]{:T(128)}, f32[8192,64]{1,0:T(8,128)}, ...), condition=%wide.region_4.5_spmd.clone.clone, body=%wide.region_0.4_spmd.clone.clone.sunk | while | flops 740347392 | bytes 150560112 | solution.py:124
  232.3 2.7 sub.510
  236.3 2.7 sub.507
  240.4 2.7 div.182
  244.7 2.7 sub.515
  248.4 2.7 sub.512
  252.1 2.7 sub.509
  254.8 2.2 exponential_divide_fusion.2
  258.3 2.7 reshape.514
  263.3 2.9 add.532
  268.0 193.3 %gather_fusion = bf16[55296,64]{1,0:T(8,128)(2,1)} fusion(bf16[8192,64]{1,0:T(8,128)(2,1)S(1)} %get-tuple-element.747, s32[55296]{0:T(1024)S(1)} %broadcast_clamp_fusion.2), kind=kCustom, calls=%fused_computation.clone.clone.1 | custom fusion | bytes 14376960 | tf_op jit(solution)/shard_map/while/body/eval_jaxpr/jit(_take)/gather | solution.py:87
  461.3 23.1 %reshape.515 = bf16[2048,27,64]{2,1,0:T(8,128)(2,1)} reshape(bf16[55296,64]{1,0:T(8,128)(2,1)} %gather_fusion) | data formatting | bytes 14155776 | tf_op jit(solution)/shard_map/while/body/eval_jaxpr/jit(_take)/gather | solution.py:87
  484.4 21.9 %multiply_reduce_fusion.2 = bf16[2048,64]{1,0:T(8,128)(2,1)S(1)} fusion(bf16[2048,27,64]{2,1,0:T(8,128)(2,1)} %reshape.515, f32[2048,27]{1,0:T(8,128)S(1)} %copy.75, pred[2048,27]{1,0:T(8,128)(4,1)} %compare_and_fusion.2), kind=kLoop, calls=%fused_computation.7.clone.1 | loop fusion | flops 14024704 | bytes 7616512 | tf_op jit(solution)/shard_map/while/body/eval_jaxpr/reduce_sum | solution.py:88
  510.3 3.0 fusion.112
  515.2 2.3 copy.76
  517.4 2.3 constant_dynamic-update-slice_fusion.5
  519.7 11.0 mul.432
  530.8 31.6 %mul.433 = f32[55296,64]{1,0:T(8,128)} reshape(f32[2048,27,64]{2,1,0:T(8,128)} %mul.432) | data formatting | bytes 28311552 | tf_op jit(solution)/shard_map/while/body/eval_jaxpr/mul | solution.py:113
  562.4 296.1 %scatter_custom_fusion.6 = f32[8192,64]{1,0:T(8,128)} fusion(f32[8192,64]{1,0:T(8,128)} %get-tuple-element.721, s32[55296]{0:T(1024)} %bitcast.91, f32[55296,64]{1,0:T(8,128)} %mul.433, f32[55296]{0:T(1024)S(1)} %copy-done.2), kind=kCustom, calls=%fused_computation.8.clone.1 | custom fusion | flops 7077888 | bytes 30629888 | tf_op jit(solution)/shard_map/while/body/eval_jaxpr/scatter-add | solution.py:114
  868.4 2.7 sub.510
  872.4 2.7 sub.507
  876.4 2.7 div.182
  880.8 2.7 sub.515
  884.5 2.7 sub.512
  888.2 2.7 sub.509
  890.9 2.2 exponential_divide_fusion.2
  894.4 2.7 reshape.514
  899.4 2.9 add.532
  904.1 193.3 %gather_fusion = bf16[55296,64]{1,0:T(8,128)(2,1)} fusion(bf16[8192,64]{1,0:T(8,128)(2,1)S(1)} %get-tuple-element.747, s32[55296]{0:T(1024)S(1)} %broadcast_clamp_fusion.2), kind=kCustom, calls=%fused_computation.clone.clone.1 | custom fusion | bytes 14376960 | tf_op jit(solution)/shard_map/while/body/eval_jaxpr/jit(_take)/gather | solution.py:87
  1097.4 23.1 %reshape.515 = bf16[2048,27,64]{2,1,0:T(8,128)(2,1)} reshape(bf16[55296,64]{1,0:T(8,128)(2,1)} %gather_fusion) | data formatting | bytes 14155776 | tf_op jit(solution)/shard_map/while/body/eval_jaxpr/jit(_take)/gather | solution.py:87
  1120.5 21.9 %multiply_reduce_fusion.2 = bf16[2048,64]{1,0:T(8,128)(2,1)S(1)} fusion(bf16[2048,27,64]{2,1,0:T(8,128)(2,1)} %reshape.515, f32[2048,27]{1,0:T(8,128)S(1)} %copy.75, pred[2048,27]{1,0:T(8,128)(4,1)} %compare_and_fusion.2), kind=kLoop, calls=%fused_computation.7.clone.1 | loop fusion | flops 14024704 | bytes 7616512 | tf_op jit(solution)/shard_map/while/body/eval_jaxpr/reduce_sum | solution.py:88
  1146.3 3.0 fusion.112
  1151.3 2.3 copy.76
  1153.5 2.3 constant_dynamic-update-slice_fusion.5
  1155.8 11.0 mul.432
  1166.9 31.6 %mul.433 = f32[55296,64]{1,0:T(8,128)} reshape(f32[2048,27,64]{2,1,0:T(8,128)} %mul.432) | data formatting | bytes 28311552 | tf_op jit(solution)/shard_map/while/body/eval_jaxpr/mul | solution.py:113
  1198.5 296.1 %scatter_custom_fusion.6 = f32[8192,64]{1,0:T(8,128)} fusion(f32[8192,64]{1,0:T(8,128)} %get-tuple-element.721, s32[55296]{0:T(1024)} %bitcast.91, f32[55296,64]{1,0:T(8,128)} %mul.433, f32[55296]{0:T(1024)S(1)} %copy-done.2), kind=kCustom, calls=%fused_computation.8.clone.1 | custom fusion | flops 7077888 | bytes 30629888 | tf_op jit(solution)/shard_map/while/body/eval_jaxpr/scatter-add | solution.py:114
  1494.8 2.4 convert_element_type.94
  1497.2 3.6 reshape.492
  1500.8 8.3 reduce.10
  1510.7 4.6 all-to-all-start.2
  1515.3 19.0 %all-to-all-done.2 = bf16[128,2,2048]{2,1,0:T(2,128)(2,1)S(1)} async-done(((bf16[128,2,2048]{2,1,0:T(2,128)(2,1)}), bf16[128,2,2048]{2,1,0:T(2,128)(2,1)S(1)}, u32[]{:S(2)}, u32[]{:S(2)}) %all-to-all-start.2) | async-done | bytes 1048608 | tf_op jit(solution)/shard_map/all_to_all | solution.py:137
  1535.4 2.6 copy.69
  1539.8 2.5 reshape.457
  (170 shorter events, 90.6 us)
Async XLA Ops:
  0.6 74.8 %copy-start = (bf16[64,1728]{1,0:T(8,128)(2,1)S(1)}, bf16[64,1728]{1,0:T(8,128)(2,1)}, u32[]{:S(2)}) copy-start(bf16[64,1728]{1,0:T(8,128)(2,1)} %param.13) | copy-start | bytes 663556
  1.5 16.7 %collective-permute-start = (bf16[1,16,1024]{2,1,0:T(8,128)(2,1)S(1)}, bf16[1,16,1024]{2,1,0:T(8,128)(2,1)S(1)}, u32[]{:S(2)}, u32[]{:S(2)}) collective-permute-start(bf16[1,16,1024]{2,1,0:T(8,128)(2,1)S(1)} %get-tuple-element.607), channel_id=1, source_target_pairs={{0,16},{16,32},{32,48},{48,64},{64,80},{80,96},{96,112},{1,17},{17... | collective-permute-start | bytes 98312 | tf_op jit(solution)/shard_map/ppermute | solution.py:15
  4.1 22.1 %all-to-all-start = ((s32[128,1,1]{2,1,0:T(1,128)}), s32[128,1,1]{2,1,0:T(1,128)S(1)}, u32[]{:S(2)}, u32[]{:S(2)}) async-start(s32[128,1,1]{2,1,0:T(1,128)} %copy.50), calls=%async_computation | async-start | bytes 131072 | tf_op jit(solution)/shard_map/all_to_all | solution.py:129
  16.9 3.1 collective-permute-start.1
  20.1 10.8 collective-permute-start.2
  23.0 8.0 collective-permute-start.3
  83.6 19.3 %collective-permute-start.4 = (bf16[1,16,1024]{2,1,0:T(8,128)(2,1)S(1)}, bf16[1,16,1024]{2,1,0:T(8,128)(2,1)S(1)}, u32[]{:S(2)}, u32[]{:S(2)}) collective-permute-start(bf16[1,16,1024]{2,1,0:T(8,128)(2,1)S(1)} %get-tuple-element.604), channel_id=1, source_target_pairs={{0,16},{16,32},{32,48},{48,64},{64,80},{80,96},{96,112},{1,17},{17... | collective-permute-start | bytes 98312 | tf_op jit(solution)/shard_map/ppermute | solution.py:15
  85.8 17.1 %collective-permute-start.5 = (bf16[1,16,1024]{2,1,0:T(8,128)(2,1)S(1)}, bf16[1,16,1024]{2,1,0:T(8,128)(2,1)S(1)}, u32[]{:S(2)}, u32[]{:S(2)}) collective-permute-start(bf16[1,16,1024]{2,1,0:T(8,128)(2,1)S(1)} %get-tuple-element.605), channel_id=1, source_target_pairs={{16,0},{32,16},{48,32},{64,48},{80,64},{96,80},{112,96},{17,1},{33... | collective-permute-start | bytes 98312 | tf_op jit(solution)/shard_map/ppermute | solution.py:18
  103.0 6.8 collective-permute-start.6
  107.3 6.9 collective-permute-start.7
  127.8 31.0 %copy-start.7 = (bf16[64,1728]{1,0:T(8,128)(2,1)S(1)}, bf16[64,1728]{1,0:T(8,128)(2,1)}, u32[]{:S(2)}) copy-start(bf16[64,1728]{1,0:T(8,128)(2,1)} %param.14) | copy-start | bytes 663556
  173.0 16.0 %copy-start.3 = (bf16[320,256]{1,0:T(8,128)(2,1)S(1)}, bf16[320,256]{1,0:T(8,128)(2,1)}, u32[]{:S(2)}) copy-start(bf16[320,256]{1,0:T(8,128)(2,1)} %param.15) | copy-start | bytes 491524
  174.6 33.5 %all-to-all-start.1 = ((bf16[128,2,2048]{2,1,0:T(2,128)(2,1)}), bf16[128,2,2048]{2,1,0:T(2,128)(2,1)S(1)}, u32[]{:S(2)}, u32[]{:S(2)}) async-start(bf16[128,2,2048]{2,1,0:T(2,128)(2,1)} %reshape.500), calls=%async_computation.1 | async-start | bytes 2097152 | tf_op jit(solution)/shard_map/all_to_all | solution.py:133
  220.0 2.3 slice-start
  222.4 5.3 copy-start.14
  222.4 5.3 copy-start.16
  222.5 5.2 copy-start.8
  222.5 5.2 copy-start.12
  224.4 3.4 copy-start.5
  232.3 6.7 copy-start.6
  239.0 8.3 copy-start.15
  243.0 8.1 copy-start.13
  251.1 5.9 copy-start.9
  506.3 1.6 copy-start.4
  507.9 0.8 copy-start.10
  508.7 1.5 copy-start.18
  508.8 1.5 copy-start.19
  510.2 3.1 copy-start.11
  530.8 31.6 %copy-start.2 = (f32[55296]{0:T(1024)S(1)}, f32[55296]{0:T(1024)}, u32[]{:S(2)}) copy-start(f32[55296]{0:T(1024)} %exponential_divide_fusion.2) | copy-start | bytes 663556 | tf_op jit(solution)/shard_map/while
  858.5 5.3 copy-start.14
  858.5 5.3 copy-start.16
  858.5 5.2 copy-start.8
  858.6 5.2 copy-start.12
  860.4 3.4 copy-start.5
  868.4 6.7 copy-start.6
  875.1 8.3 copy-start.15
  879.1 8.1 copy-start.13
  887.2 5.9 copy-start.9
  1142.4 1.6 copy-start.4
  1144.0 0.8 copy-start.10
  1144.8 1.5 copy-start.18
  1144.8 1.5 copy-start.19
  1146.3 3.1 copy-start.11
  1166.9 31.6 %copy-start.2 = (f32[55296]{0:T(1024)S(1)}, f32[55296]{0:T(1024)}, u32[]{:S(2)}) copy-start(f32[55296]{0:T(1024)} %exponential_divide_fusion.2) | copy-start | bytes 663556 | tf_op jit(solution)/shard_map/while
  1510.7 23.7 %all-to-all-start.2 = ((bf16[128,2,2048]{2,1,0:T(2,128)(2,1)}), bf16[128,2,2048]{2,1,0:T(2,128)(2,1)S(1)}, u32[]{:S(2)}, u32[]{:S(2)}) async-start(bf16[128,2,2048]{2,1,0:T(2,128)(2,1)} %reshape.502), calls=%async_computation.2 | async-start | bytes 2097152 | tf_op jit(solution)/shard_map/all_to_all | solution.py:137
  1535.4 2.7 copy-start.17
  1539.2 3.0 copy-start.1
where the time goes:
time: 1560 us; the launch traced here: 1540 us
  local copies, waits for them, and re-layouts  719 us (46%)
  other arithmetic  688 us (44%)
  starting transfers between devices  58.2 us (4%)
  waiting for transfers between devices  45.1 us (3%)
  matrix products  30.2 us (2%)
    scatter-add x2, other arithmetic, advance(): partial_value.at[targets.reshape(-1)].add(spread.reshape(-1, channels))  592 us
    gather x4, local copies, waits for them, and re-layouts, advance(): picked = jnp.take(cell_rows, targets, axis=0)  433 us
    mul x4, local copies, waits for them, and re-layouts, advance(): spread = weights[:, :, None] * grad_sampled[:, None, :]  85.3 us
    concatenate x2, local copies, waits for them, and re-layouts, conv_core(): stacked = jnp.concatenate(pieces, axis=-1).reshape(-1, 27 * channels)  61.9 us
    reduce_sum x2, other arithmetic, advance(): jnp.sum(weights[:, :, None] * picked.astype(jnp.float32), axis=1)  43.8 us
  transfers between devices with their start and end apart: 11, of which 6 were waited for; matrix products, arithmetic and copies ran while one was open for 1% of the time, Pallas kernels for 0%

commit v1 on v0

v1 whole, which is shorter than its diff:
```python
import functools

import jax
import jax.numpy as jnp
from jax import lax
from jax.experimental import pallas as pl
from jax.experimental.pallas import tpu as pltpu
from jax.sharding import PartitionSpec as P

PB = 512

def gelu_pair(x):
    k = 0.7978845608028654
    c = 0.044715
    x2 = x * x
    t = jnp.tanh(k * x * (1.0 + c * x2))
    half = 0.5 * (1.0 + t)
    value = x * half
    slope = half + 0.5 * x * (1.0 - t * t) * (k * (1.0 + 3.0 * c * x2))
    return value, slope

def decode_kernel(x_ref, anchor_ref, frac_ref, feat_ref, cot_ref, w_in_ref, w_out_ref,
                  pred_ref, fg_ref, part_ref, xt_ref, wt_ref, wo_ref, a_ref, acc_ref):
    step = pl.program_id(0)
    slots = x_ref.shape[0] // 16
    pb = anchor_ref.shape[1]

    @pl.when(step == 0)
    def _():
        xt_ref[...] = x_ref[...].T
        wt_ref[...] = w_in_ref[...].T
        wo = w_out_ref[...].astype(jnp.float32).T
        wo_ref[...] = jnp.concatenate([wo, wo, wo, jnp.zeros_like(wo)], axis=1).astype(jnp.bfloat16)
        acc_ref[...] = jnp.zeros_like(acc_ref)

    anchor = anchor_ref[...]
    slot = anchor >> 6
    cell = lax.broadcasted_iota(jnp.int32, (16, pb), 0)
    off_x = (cell >> 2) - ((anchor >> 4) & 3)
    off_y = (cell & 3) - ((anchor >> 2) & 3)
    off_z = lax.broadcasted_iota(jnp.int32, (4, pb), 0) - (anchor & 3)
    dist_x = frac_ref[0:1, :] - off_x.astype(jnp.float32)
    dist_y = frac_ref[1:2, :] - off_y.astype(jnp.float32)
    dist_z = frac_ref[2:3, :] - off_z.astype(jnp.float32)
    near = jnp.logical_and(jnp.abs(off_x) <= 1, jnp.abs(off_y) <= 1)
    kxy = jnp.where(near, jnp.exp(-(dist_x * dist_x + dist_y * dist_y)), 0.0)
    kz = jnp.where(jnp.abs(off_z) <= 1, jnp.exp(-(dist_z * dist_z)), 0.0)
    wxy = (kxy / jnp.sum(kxy, axis=0, keepdims=True)).astype(jnp.bfloat16)
    wz = kz / jnp.sum(kz, axis=0, keepdims=True)

    slot16 = jnp.broadcast_to(slot.astype(jnp.float32), (16, pb)).astype(jnp.bfloat16)
    zero = jnp.zeros_like(wxy)
    for s in range(slots):
        a_ref[s * 16 : (s + 1) * 16, :] = jnp.where(slot16 == jnp.bfloat16(s), wxy, zero)

    mixed = jnp.dot(xt_ref[...], a_ref[...], preferred_element_type=jnp.float32)
    sampled = mixed[0:64] * wz[0:1] + mixed[64:128] * wz[1:2] + mixed[128:192] * wz[2:3] + mixed[192:256] * wz[3:4]
    sampled = sampled.astype(jnp.bfloat16)
    preact = jnp.dot(wt_ref[:, 64:], feat_ref[...], preferred_element_type=jnp.float32) + jnp.dot(
        wt_ref[:, :64], sampled, preferred_element_type=jnp.float32)
    value, slope = gelu_pair(preact)
    pred_ref[...] = jnp.dot(w_out_ref[...], value.astype(jnp.bfloat16), preferred_element_type=jnp.float32)
    cot = cot_ref[...]
    hi = cot.astype(jnp.bfloat16).astype(jnp.float32)
    rest = cot - hi
    mid = rest.astype(jnp.bfloat16).astype(jnp.float32)
    low = rest - mid
    pieces = jnp.concatenate([hi, mid, low, jnp.zeros_like(hi)], axis=0).astype(jnp.bfloat16)
    grad_active = jnp.dot(wo_ref[...], pieces, preferred_element_type=jnp.float32)
    grad_pre = (grad_active * slope).astype(jnp.bfloat16)
    back = jnp.dot(w_in_ref[...], grad_pre, preferred_element_type=jnp.float32)
    fg_ref[...] = back[64:].astype(jnp.bfloat16)
    grad_sampled = back[:64]
    spread = jnp.concatenate([grad_sampled * wz[i : i + 1] for i in range(4)], axis=0).astype(jnp.bfloat16)
    acc_ref[...] += lax.dot_general(a_ref[...], spread, (((1,), (1,)), ((), ())), preferred_element_type=jnp.float32)

    @pl.when(step == pl.num_programs(0) - 1)
    def _():
        part_ref[...] = acc_ref[...].astype(jnp.bfloat16)


def decode(x, anchor, frac, feat, cot, w_in, w_out, interpret=False):
    count = anchor.shape[1]
    rows = x.shape[0]
    whole = lambda a: pl.BlockSpec(a.shape, lambda i: (0, 0))
    col = lambda r: pl.BlockSpec((r, PB), lambda i: (0, i))
    return pl.pallas_call(
        decode_kernel,
        grid=(count // PB,),
        in_specs=[whole(x), col(1), col(3), col(256), col(4), whole(w_in), whole(w_out)],
        out_specs=[col(4), col(256), pl.BlockSpec((rows, 256), lambda i: (0, 0))],
        out_shape=[jax.ShapeDtypeStruct((4, count), jnp.float32), jax.ShapeDtypeStruct((256, count), jnp.bfloat16),
                   jax.ShapeDtypeStruct((rows, 256), jnp.bfloat16)],
        scratch_shapes=[pltpu.VMEM((256, rows), jnp.bfloat16), pltpu.VMEM((256, 320), jnp.bfloat16),
                        pltpu.VMEM((256, 16), jnp.bfloat16), pltpu.VMEM((rows, PB), jnp.bfloat16), pltpu.VMEM((rows, 256), jnp.float32)],
        compiler_params=pltpu.CompilerParams(vmem_limit_bytes=48 << 20),
        interpret=interpret,
        name="decode",
    )(x, anchor, frac, feat, cot, w_in, w_out)


def gelu(x):
    return 0.5 * x * (1.0 + jnp.tanh(0.7978845608028654 * x * (1.0 + 0.044715 * (x * x))))


def pad_z(v):
    gap = jnp.zeros((v.shape[0], 64), v.dtype)
    return jnp.concatenate([gap, v, gap], axis=1)


def spread_weight(w_ref, band_ref):
    for k in range(9):
        tap = w_ref[:, k * 192 : (k + 1) * 192]
        for j in range(4):
            parts = [jnp.zeros((64, j * 64), tap.dtype)] * (j > 0) + [tap] + [jnp.zeros((64, 192 - j * 64), tap.dtype)] * (j < 3)
            band_ref[j * 64 : (j + 1) * 64, k * 384 : (k + 1) * 384] = jnp.concatenate(parts, axis=1)


def shift_rows(stack_ref, index, tile, low, high):
    stack_ref[0, index] = jnp.concatenate([low, tile[:15]], axis=0).astype(jnp.bfloat16)
    stack_ref[1, index] = tile.astype(jnp.bfloat16)
    stack_ref[2, index] = jnp.concatenate([tile[1:], high], axis=0).astype(jnp.bfloat16)


def conv_kernel(pos_ref, table_ref, latent_ref, cols_ref, hx_ref, hy_ref, hc_ref, w1_ref, w2_ref, out_ref,
                band1_ref, band2_ref, rows_ref, edge_ref, hid_ref, hcol_ref, tiles_ref, *, n_gx, n_gy):
    f32 = jnp.float32
    gx, gy = pos_ref[0], pos_ref[1]
    left, right = gx > 0, gx < n_gx - 1
    down, up = gy > 0, gy < n_gy - 1
    x_side, y_side = (left, right), (down, up)
    spread_weight(w1_ref, band1_ref)
    spread_weight(w2_ref, band2_ref)

    def halo_col(side, j):
        mid = hy_ref[side, j].astype(f32)
        low = jnp.where(left, hc_ref[0, side, j].astype(f32), 0.0)
        high = jnp.where(right, hc_ref[1, side, j].astype(f32), 0.0)
        return pad_z(jnp.where(y_side[side], jnp.concatenate([low, mid, high], axis=0), 0.0))

    def own_col(y, c):
        low = [hx_ref[0, i, y : y + 1, :].astype(f32) for i in range(2)]
        high = [hx_ref[1, i, y : y + 1, :].astype(f32) for i in range(2)]
        low = jnp.where(left, jnp.concatenate(low, axis=0), 0.0)
        high = jnp.where(right, jnp.concatenate(high, axis=0), 0.0)
        return pad_z(jnp.concatenate([low, cols_ref[c].astype(f32), high], axis=0))

    lower = [halo_col(0, 0), halo_col(0, 1), own_col(0, 0)]
    upper = [own_col(15, 3), halo_col(1, 0), halo_col(1, 1)]
    fill = jnp.zeros((6, 1152), f32)
    for dx in range(3):
        for dy in range(3):
            edge_ref[dx * 3 + dy] = jnp.concatenate(
                [lower[dy][dx : dx + 18], fill, upper[dy][dx : dx + 18], fill], axis=0).astype(jnp.bfloat16)
    for x in range(20):
        if x < 2:
            tile = jnp.where(left, hx_ref[0, x].astype(f32), 0.0)
        elif x < 18:
            tile = latent_ref[x - 2].astype(f32)
        else:
            tile = jnp.where(right, hx_ref[1, x - 18].astype(f32), 0.0)
        shift_rows(rows_ref, x, pad_z(tile), lower[1][x : x + 1], upper[1][x : x + 1])

    row24 = lax.broadcasted_iota(jnp.int32, (24, 1), 0)
    inside = jnp.logical_and(jnp.logical_or(row24 > 0, left), jnp.logical_or(row24 != 17, right))

    for b in range(4):
        lanes = slice(b * 256, b * 256 + 384)
        taps = []
        for dx in range(3):
            for dy in range(3):
                taps.append(jnp.concatenate([rows_ref[dy, dx : dx + 18, :, lanes].reshape(288, 384), edge_ref[dx * 3 + dy, :, lanes]], axis=0))
        acc = lax.dot_general(jnp.concatenate(taps, axis=1), band1_ref[...], (((1,), (1,)), ((), ())), preferred_element_type=f32)
        acc = gelu(acc)
        out = slice(b * 256, b * 256 + 256)
        hid_ref[0, :, out] = jnp.where(left, acc[:16], 0.0)
        hid_ref[1:17, :, out] = acc[16:272].reshape(16, 16, 256)
        hid_ref[17, :, out] = jnp.where(right, acc[272:288], 0.0)
        hcol_ref[0, :, out] = jnp.where(jnp.logical_and(inside, down), acc[288:312], 0.0)
        hcol_ref[1, :, out] = jnp.where(jnp.logical_and(inside, up), acc[312:336], 0.0)

    low, high = pad_z(hcol_ref[0]), pad_z(hcol_ref[1])
    for x in range(18):
        shift_rows(rows_ref, x, pad_z(hid_ref[x]), low[x : x + 1], high[x : x + 1])

    for b in range(4):
        lanes = slice(b * 256, b * 256 + 384)
        taps = [rows_ref[dy, dx : dx + 16, :, lanes].reshape(256, 384) for dx in range(3) for dy in range(3)]
        acc = lax.dot_general(jnp.concatenate(taps, axis=1), band2_ref[...], (((1,), (1,)), ((), ())), preferred_element_type=f32)
        acc = acc.reshape(16, 16, 256) + latent_ref[:, :, b * 256 : b * 256 + 256].astype(f32)
        for tx in range(4):
            for ty in range(4):
                tile = [acc[tx * 4 + i, ty * 4 : ty * 4 + 4] for i in range(4)]
                tiles_ref[(tx * 4 + ty) * 4 + b] = jnp.concatenate(tile, axis=0).astype(jnp.bfloat16)

    me = gx * n_gy + gy

    def pick(d, carry):
        wanted = table_ref[d, 0, me]
        tile = tiles_ref[jnp.maximum(wanted, 0)]
        out_ref[d] = jnp.where(wanted >= 0, tile, jnp.zeros_like(tile))
        return carry

    lax.fori_loop(0, out_ref.shape[0], pick, 0, unroll=8)


def convolve(pos, table, latent, cols, hx, hy, hc, w1, w2, n_gx, n_gy, interpret=False):
    vm = pl.BlockSpec(memory_space=pltpu.VMEM)
    sm = pl.BlockSpec(memory_space=pltpu.SMEM)
    bf, f32 = jnp.bfloat16, jnp.float32
    return pl.pallas_call(
        functools.partial(conv_kernel, n_gx=n_gx, n_gy=n_gy),
        in_specs=[sm, sm] + [vm] * 7,
        out_specs=vm,
        out_shape=jax.ShapeDtypeStruct((n_gx * n_gy, 16, 256), bf),
        scratch_shapes=[pltpu.VMEM((256, 3456), bf), pltpu.VMEM((256, 3456), bf), pltpu.VMEM((3, 20, 16, 1152), bf),
                        pltpu.VMEM((9, 48, 1152), bf), pltpu.VMEM((18, 16, 1024), f32), pltpu.VMEM((2, 24, 1024), f32),
                        pltpu.VMEM((64, 16, 256), bf)],
        compiler_params=pltpu.CompilerParams(vmem_limit_bytes=48 << 20),
        interpret=interpret,
        name="convolve",
    )(pos, table, latent, cols, hx, hy, hc, w1, w2)


def collect_kernel(pos_ref, table_ref, back_ref, out_ref, sum_ref, *, n_gy):
    me = pos_ref[0] * n_gy + pos_ref[1]
    sum_ref[...] = jnp.zeros_like(sum_ref)

    def add(d, carry):
        wanted = table_ref[d, 0, me]
        row = jnp.where(wanted >= 0, wanted, 64)
        sum_ref[row] += back_ref[d].astype(jnp.float32)
        return carry

    lax.fori_loop(0, back_ref.shape[0], add, 0, unroll=8)
    for tx in range(4):
        for ty in range(4):
            for tz in range(4):
                tile = sum_ref[(tx * 4 + ty) * 4 + tz]
                for i in range(4):
                    out_ref[tx * 4 + i, ty * 4 : ty * 4 + 4, tz * 256 : tz * 256 + 256] = tile[i * 4 : i * 4 + 4]


def collect(pos, table, back, n_gy, interpret=False):
    vm = pl.BlockSpec(memory_space=pltpu.VMEM)
    sm = pl.BlockSpec(memory_space=pltpu.SMEM)
    return pl.pallas_call(
        functools.partial(collect_kernel, n_gy=n_gy),
        in_specs=[sm, sm, vm],
        out_specs=vm,
        out_shape=jax.ShapeDtypeStruct((16, 16, 1024), jnp.float32),
        scratch_shapes=[pltpu.VMEM((65, 16, 256), jnp.float32)],
        compiler_params=pltpu.CompilerParams(vmem_limit_bytes=32 << 20),
        interpret=interpret,
        name="collect",
    )(pos, table, back)


MESH = pl.DeviceIdType.MESH


def peer_of(k, n_gx, n_gy):
    gx, gy = lax.axis_index("gx"), lax.axis_index("gy")
    index = lax.rem(gx * n_gy + gy + k, n_gx * n_gy)
    return index, (index // n_gy, lax.rem(index, n_gy))


def greet_all(n_gx, n_gy):
    barrier = pltpu.get_barrier_semaphore()
    count = n_gx * n_gy

    def signal(k, carry):
        pl.semaphore_signal(barrier, inc=1, device_id=peer_of(k, n_gx, n_gy)[1], device_id_type=MESH)
        return carry

    lax.fori_loop(1, count, signal, 0)
    pl.semaphore_wait(barrier, count - 1)


def trade(source_of, target_ref, own, own_sem, send_sem, recv_sem, n_gx, n_gy):
    count = n_gx * n_gy
    me = lax.axis_index("gx") * n_gy + lax.axis_index("gy")

    def send(k, carry):
        index, device = peer_of(k, n_gx, n_gy)
        pltpu.make_async_remote_copy(src_ref=source_of(index), dst_ref=target_ref.at[me], send_sem=send_sem, recv_sem=recv_sem,
                                     device_id=device, device_id_type=MESH).start()
        return carry

    lax.fori_loop(1, count, send, 0)
    local = pltpu.make_async_copy(own, target_ref.at[me], own_sem)
    local.start()
    return local


def finish(target_ref, local, send_sem, recv_sem, count):
    others = target_ref.at[pl.ds(0, count - 1)]
    local.wait()
    pltpu.make_async_copy(others, others, send_sem).wait()
    pltpu.make_async_copy(others, others, recv_sem).wait()


def swap_kernel(out_ref, in_ref, own_sem, send_sem, recv_sem, *, n_gx, n_gy):
    me = lax.axis_index("gx") * n_gy + lax.axis_index("gy")
    greet_all(n_gx, n_gy)
    local = trade(lambda index: out_ref.at[index], in_ref, out_ref.at[me], own_sem, send_sem, recv_sem, n_gx, n_gy)
    finish(in_ref, local, send_sem, recv_sem, n_gx * n_gy)


def swap(outgoing, n_gx, n_gy, collective_id):
    hbm = pl.BlockSpec(memory_space=pl.ANY)
    dma = pltpu.SemaphoreType.DMA
    return pl.pallas_call(
        functools.partial(swap_kernel, n_gx=n_gx, n_gy=n_gy),
        in_specs=[hbm],
        out_specs=hbm,
        out_shape=jax.ShapeDtypeStruct(outgoing.shape, outgoing.dtype),
        scratch_shapes=[dma(()), dma(()), dma(())],
        compiler_params=pltpu.CompilerParams(collective_id=collective_id, has_side_effects=True),
        name="swap",
    )(outgoing)


def border_kernel(latent_ref, cols_ref, corner_ref, touch_ref, hx_ref, hy_ref, hc_ref, table_ref, pos_ref,
                  own_sem, send_sem, recv_sem, side_send, side_recv, *, n_gx, n_gy):
    gx, gy = lax.axis_index("gx"), lax.axis_index("gy")
    pos_ref[0] = gx
    pos_ref[1] = gy
    greet_all(n_gx, n_gy)
    low_x, high_x = lax.rem(gx + n_gx - 1, n_gx), lax.rem(gx + 1, n_gx)
    low_y, high_y = lax.rem(gy + n_gy - 1, n_gy), lax.rem(gy + 1, n_gy)
    moves = [
        (latent_ref.at[pl.ds(0, 2)], hx_ref.at[1], (low_x, gy)),
        (latent_ref.at[pl.ds(14, 2)], hx_ref.at[0], (high_x, gy)),
        (cols_ref.at[pl.ds(0, 2)], hy_ref.at[1], (gx, low_y)),
        (cols_ref.at[pl.ds(2, 2)], hy_ref.at[0], (gx, high_y)),
    ]
    for i, near_x in enumerate((low_x, high_x)):
        for j, near_y in enumerate((low_y, high_y)):
            moves.append((corner_ref.at[i, j], hc_ref.at[1 - i, 1 - j], (near_x, near_y)))
    copies = []
    for m, (source, target, device) in enumerate(moves):
        copies.append(pltpu.make_async_remote_copy(src_ref=source, dst_ref=target, send_sem=side_send.at[m], recv_sem=side_recv.at[m],
                                                   device_id=device, device_id_type=MESH))
    for copy in copies:
        copy.start()
    local = trade(lambda index: touch_ref.at[0], table_ref, touch_ref.at[0], own_sem, send_sem, recv_sem, n_gx, n_gy)
    for copy in copies:
        copy.wait()
    finish(table_ref, local, send_sem, recv_sem, n_gx * n_gy)


def border(latent, cols, corner, touch, n_gx, n_gy, collective_id):
    hbm = pl.BlockSpec(memory_space=pl.ANY)
    dma = pltpu.SemaphoreType.DMA
    bf = latent.dtype
    width = latent.shape[2]
    shapes = [((2, 2, 16, width), bf), ((2, 2, 16, width), bf), ((2, 2, 2, 2, width), bf),
              ((n_gx * n_gy, 1, n_gx * n_gy), jnp.int32), ((2,), jnp.int32)]
    return pl.pallas_call(
        functools.partial(border_kernel, n_gx=n_gx, n_gy=n_gy),
        in_specs=[hbm] * 4,
        out_specs=[hbm] * 4 + [pl.BlockSpec(memory_space=pltpu.SMEM)],
        out_shape=[jax.ShapeDtypeStruct(s, d) for s, d in shapes],
        scratch_shapes=[dma(()), dma(()), dma(()), dma((8,)), dma((8,))],
        compiler_params=pltpu.CompilerParams(collective_id=collective_id, has_side_effects=True),
        name="border",
    )(latent, cols, corner, touch)


def make_body(n_gx, n_gy):
    def body(latent, conv_first, conv_second, w_in, w_out, touch, anchor, frac, pfeat, cotangent):
        width = latent.shape[2]
        cols = jnp.stack([latent[:, 0], latent[:, 1], latent[:, 14], latent[:, 15]])
        corner = jnp.stack([jnp.stack([cols[2 * j : 2 * j + 2, 14 * i : 14 * i + 2] for j in range(2)]) for i in range(2)])
        hx, hy, hc, table, pos = border(latent, cols, corner, touch.reshape(1, 1, -1), n_gx, n_gy, 0)
        outgoing = convolve(pos, table, latent, cols, hx, hy, hc, conv_first, conv_second, n_gx, n_gy)
        received = swap(outgoing, n_gx, n_gy, 1)
        predicted, feature_grads, partial_sums = decode(
            received.reshape(-1, 256), anchor.reshape(1, -1), frac, pfeat, cotangent, w_in, w_out)
        returned = swap(partial_sums.reshape(received.shape), n_gx, n_gy, 2)
        grid_grad = collect(pos, table, returned, n_gy)
        return (predicted, feature_grads, grid_grad)

    return body


def solution(mesh):
    rows = P(("gx", "gy"), None)
    cols = P(None, ("gx", "gy"))
    grid = P("gx", "gy", None)
    return jax.shard_map(
        make_body(mesh.shape["gx"], mesh.shape["gy"]),
        mesh=mesh,
        in_specs=(grid, P(), P(), P(), P(), rows, P(("gx", "gy")), cols, cols, cols),
        out_specs=(cols, cols, grid),
        check_vma=False,
    )
```

time: 1560 us -> 107 us (0.07)
  the two profiles are of different devices: /device:TPU:0 before, /device:TPU:1 now
where the time goes in v1:
time: 107 us; the launch traced here: 106 us
  Pallas kernels  93.2 us (87%)
  local copies, waits for them, and re-layouts  10.9 us (10%)
  other arithmetic  1.43 us (1%)
    pallas_call x2, Pallas kernels, swap(): pl.pallas_call(functools.partial(swap_kernel, n_gx=n_gx, n_gy=n_gy), in_s...  43 us
    pallas_call x1, Pallas kernels, decode(): pl.pallas_call(decode_kernel, grid=(count // PB,), in_specs=[whole(x), co...  19.6 us
    pallas_call x1, Pallas kernels, border(): pl.pallas_call(functools.partial(border_kernel, n_gx=n_gx, n_gy=n_gy), in...  19.5 us
    unnamed x42, local copies, waits for them, and re-layouts  9.35 us
    pallas_call x1, Pallas kernels, convolve(): pl.pallas_call(functools.partial(conv_kernel, n_gx=n_gx, n_gy=n_gy), in_s...  7.75 us
    pallas_call x1, Pallas kernels, collect(): pl.pallas_call(functools.partial(collect_kernel, n_gy=n_gy), in_specs=[sm...  3.38 us

profile of v1, /device:TPU:1, one launch (start us, length us, event | category | flops | bytes accessed | tf_op | source)
XLA Modules:
  0.0 106.4 jit_solution(16925373081888858969)
XLA Ops:
  0.6 0.0 copy-start.3
  0.6 0.0 copy-start.10
  0.7 0.0 copy-start.9
  0.7 1.5 %fusion.2 = (bf16[16,1,1024]{2,1,0:T(2,128)(2,1)S(1)}, bf16[16,1,1024]{2,1,0:T(2,128)(2,1)S(1)}, bf16[16,1,1024]{2,1,0:T(2,128)(2,1)S(1)}, bf16[16,1,1024]{2,1,0:T(2,128)(2,1)S(1)}) fusion(bf16[16,16,1024]{2,1,0:T(8,128)(2,1)} %latent_ref.3), kind=kLoop, calls=%fused_computation.14 | loop fusion | bytes 262144 | tf_op jit(solution)/shard_map/slice | solution.py:374
  2.3 0.7 pad_maximum_fusion.cols_ref
  3.0 0.7 pad_maximum_fusion.1.corner_ref
  3.7 19.5 %border.1 = (bf16[2,2,16,1024]{3,2,1,0:T(8,128)(2,1)}, bf16[2,2,16,1024]{3,2,1,0:T(8,128)(2,1)}, bf16[2,2,2,2,1024]{4,3,2,1,0:T(2,128)(2,1)}, s32[128,1,128]{2,1,0:T(1,128)}, s32[2]{0:T(128)}) custom-call(bf16[16,16,1024]{2,1,0:T(8,128)(2,1)} %latent_ref.3, bf16[4,16,1024]{2,1,0:T(8,128)(2,1)} %pad_maximum_fusion.cols_ref, ...), custom_call_target="tpu_custom_call" | custom-call | tf_op jit(solution)/shard_map/border/pallas_call | solution.py:360
  23.2 0.0 copy-done.3
  23.2 0.0 copy-done.10
  23.2 0.0 copy-done.9
  23.2 0.0 copy-start.5
  23.2 0.9 copy-done.5
  24.1 0.0 copy-start.7
  24.1 0.8 copy-done.7
  25.0 0.0 copy-start.12
  25.0 0.9 copy-done.12
  25.9 0.0 copy-start.13
  25.9 0.9 copy-done.13
  26.8 0.0 copy-start.16
  26.8 0.8 copy-done.16
  27.5 0.0 copy-start.19
  27.5 0.6 copy-done.19
  28.2 0.0 copy-start.4
  28.2 0.0 copy-start.11
  28.2 0.0 copy-start.14
  28.2 0.0 copy-start.15
  28.2 0.0 copy-start.17
  28.2 0.0 copy-start.18
  28.2 7.7 %convolve.1.out_ref = bf16[128,16,256]{2,1,0:T(8,128)(2,1)S(1)} custom-call(s32[2]{0:T(128)S(1)} %copy-done.19, s32[128,1,128]{2,1,0:T(1,128)S(1)} %copy-done.7, bf16[16,16,1024]{2,1,0:T(8,128)(2,1)S(1)} %copy-done.3, bf16[4,16,1024]{2,1,0:T(8,128)(2,1)S(1)} %copy-done.5, bf16[2,2,16,1024]{3,2,1,0:T(8,128)(2,1)S(1)} %copy-done.12, ...), custom_call_target="tpu_custom_call" | custom-call | tf_op jit(solution)/shard_map/convolve/pallas_call | solution.py:211
  35.9 0.0 copy-start.2
  36.0 1.0 copy-done.2
  36.9 21.9 %swap.2 = bf16[128,16,256]{2,1,0:T(8,128)(2,1)} custom-call(bf16[128,16,256]{2,1,0:T(8,128)(2,1)} %copy-done.2), custom_call_target="tpu_custom_call" | custom-call | tf_op jit(solution)/shard_map/swap/pallas_call | solution.py:313
  58.8 0.0 copy-done.4
  58.8 0.0 copy-done.11
  58.8 0.0 copy-done.14
  58.9 0.0 copy-done.15
  58.9 0.0 copy-done.17
  58.9 0.0 copy-done.18
  58.9 0.0 copy-start
  58.9 1.2 %copy-done = bf16[128,16,256]{2,1,0:T(8,128)(2,1)S(1)} copy-done((bf16[128,16,256]{2,1,0:T(8,128)(2,1)S(1)}, bf16[128,16,256]{2,1,0:T(8,128)(2,1)}, u32[]{:S(2)}) %copy-start) | copy-done | bytes 1048600
  60.1 0.0 copy-start.8
  60.1 0.0 copy-start.20
  60.1 19.6 %decode.1 = (f32[4,4096]{1,0:T(4,128)}, bf16[256,4096]{1,0:T(8,128)(2,1)}, bf16[2048,256]{1,0:T(8,128)(2,1)S(1)}) custom-call(bf16[2048,256]{1,0:T(8,128)(2,1)S(1)} %bitcast.24, s32[1,4096]{1,0:T(1,128)S(1)} %bitcast.26, f32[3,4096]{1,0:T(4,128)S(1)} %copy-done.14, bf16[256,4096]{1,0:T(8,128)(2,1)S(1)} %copy-done.4, f32[4,4096]{1,0:T(4,128)S(1)} %copy-done.15, ...), custom_call_target="tpu_custom_call" | custom-call | tf_op jit(solution)/shard_map/decode/pallas_call | solution.py:87
  79.8 0.0 copy-start.6
  79.8 1.0 copy-done.6
  80.7 21.1 %swap.3.back_ref = bf16[128,16,256]{2,1,0:T(8,128)(2,1)} custom-call(bf16[128,16,256]{2,1,0:T(8,128)(2,1)} %bitcast.25), custom_call_target="tpu_custom_call" | custom-call | tf_op jit(solution)/shard_map/swap/pallas_call | solution.py:313
  101.8 0.0 copy-done.8
  101.8 0.0 copy-done.20
  101.8 0.0 copy-start.1
  101.8 1.2 %copy-done.1 = bf16[128,16,256]{2,1,0:T(8,128)(2,1)S(1)} copy-done((bf16[128,16,256]{2,1,0:T(8,128)(2,1)S(1)}, bf16[128,16,256]{2,1,0:T(8,128)(2,1)}, u32[]{:S(2)}) %copy-start.1) | copy-done | bytes 1048600
  103.0 3.4 %collect.1 = f32[16,16,1024]{2,1,0:T(8,128)} custom-call(s32[2]{0:T(128)S(1)} %copy-done.20, s32[128,1,128]{2,1,0:T(1,128)S(1)} %copy-done.8, bf16[128,16,256]{2,1,0:T(8,128)(2,1)S(1)} %copy-done.1), custom_call_target="tpu_custom_call" | custom-call | tf_op jit(solution)/shard_map/collect/pallas_call | solution.py:247
  (6 shorter events, 0.1 us)
Async XLA Ops:
  0.6 22.5 %copy-start.3 = (bf16[16,16,1024]{2,1,0:T(8,128)(2,1)S(1)}, bf16[16,16,1024]{2,1,0:T(8,128)(2,1)}, u32[]{:S(2)}) copy-start(bf16[16,16,1024]{2,1,0:T(8,128)(2,1)} %latent_ref.3) | copy-start | bytes 1572868
  0.6 22.5 %copy-start.10 = (bf16[64,1728]{1,0:T(8,128)(2,1)S(1)}, bf16[64,1728]{1,0:T(8,128)(2,1)}, u32[]{:S(2)}) copy-start(bf16[64,1728]{1,0:T(8,128)(2,1)} %w2_ref.1) | copy-start | bytes 663556
  0.7 22.5 %copy-start.9 = (bf16[64,1728]{1,0:T(8,128)(2,1)S(1)}, bf16[64,1728]{1,0:T(8,128)(2,1)}, u32[]{:S(2)}) copy-start(bf16[64,1728]{1,0:T(8,128)(2,1)} %w1_ref.1) | copy-start | bytes 663556
  23.2 0.9 copy-start.5
  24.1 0.8 copy-start.7
  25.0 0.9 copy-start.12
  25.9 0.9 copy-start.13
  26.8 0.8 copy-start.16
  27.5 0.6 copy-start.19
  28.2 30.7 %copy-start.4 = (bf16[256,4096]{1,0:T(8,128)(2,1)S(1)}, bf16[256,4096]{1,0:T(8,128)(2,1)}, u32[]{:S(2)}) copy-start(bf16[256,4096]{1,0:T(8,128)(2,1)} %feat_ref.1) | copy-start | bytes 6291460
  28.2 30.7 %copy-start.11 = (bf16[320,256]{1,0:T(8,128)(2,1)S(1)}, bf16[320,256]{1,0:T(8,128)(2,1)}, u32[]{:S(2)}) copy-start(bf16[320,256]{1,0:T(8,128)(2,1)} %w_in_ref.1) | copy-start | bytes 491524
  28.2 30.7 %copy-start.14 = (f32[3,4096]{1,0:T(4,128)S(1)}, f32[3,4096]{1,0:T(4,128)}, u32[]{:S(2)}) copy-start(f32[3,4096]{1,0:T(4,128)} %frac_ref.1) | copy-start | bytes 147460
  28.2 30.7 %copy-start.15 = (f32[4,4096]{1,0:T(4,128)S(1)}, f32[4,4096]{1,0:T(4,128)}, u32[]{:S(2)}) copy-start(f32[4,4096]{1,0:T(4,128)} %cot_ref.1) | copy-start | bytes 196612
  28.2 30.7 %copy-start.17 = (s32[4096]{0:T(1024)S(1)}, s32[4096]{0:T(1024)}, u32[]{:S(2)}) copy-start(s32[4096]{0:T(1024)} %param.16) | copy-start | bytes 49156
  28.2 30.7 %copy-start.18 = (bf16[4,256]{1,0:T(4,128)(2,1)S(1)}, bf16[4,256]{1,0:T(4,128)(2,1)}, u32[]{:S(2)}) copy-start(bf16[4,256]{1,0:T(4,128)(2,1)} %w_out_ref.1) | copy-start | bytes 6148
  35.9 1.0 copy-start.2
  58.9 1.2 %copy-start = (bf16[128,16,256]{2,1,0:T(8,128)(2,1)S(1)}, bf16[128,16,256]{2,1,0:T(8,128)(2,1)}, u32[]{:S(2)}) copy-start(bf16[128,16,256]{2,1,0:T(8,128)(2,1)} %swap.2) | copy-start | bytes 3145732
  60.1 41.7 %copy-start.8 = (s32[128,1,128]{2,1,0:T(1,128)S(1)}, s32[128,1,128]{2,1,0:T(1,128)}, u32[]{:S(2)}) copy-start(s32[128,1,128]{2,1,0:T(1,128)} %get-tuple-element.12.table_ref) | copy-start | bytes 196612
  60.1 41.7 %copy-start.20 = (s32[2]{0:T(128)S(1)}, s32[2]{0:T(128)}, u32[]{:S(2)}) copy-start(s32[2]{0:T(128)} %get-tuple-element.11.pos_ref) | copy-start | bytes 28
  79.8 1.0 copy-start.6
  101.8 1.2 %copy-start.1 = (bf16[128,16,256]{2,1,0:T(8,128)(2,1)S(1)}, bf16[128,16,256]{2,1,0:T(8,128)(2,1)}, u32[]{:S(2)}) copy-start(bf16[128,16,256]{2,1,0:T(8,128)(2,1)} %swap.3.back_ref) | copy-start | bytes 3145732

commit v2 on v1

v2 whole, which is shorter than its diff:
```python
import functools

import jax
import jax.numpy as jnp
from jax import lax
from jax.experimental import pallas as pl
from jax.experimental.pallas import tpu as pltpu
from jax.sharding import PartitionSpec as P


def gelu_pair(x):
    k = 0.7978845608028654
    c = 0.044715
    x2 = x * x
    t = jnp.tanh(k * x * (1.0 + c * x2))
    half = 0.5 * (1.0 + t)
    value = x * half
    slope = half + 0.5 * x * (1.0 - t * t) * (k * (1.0 + 3.0 * c * x2))
    return value, slope


def gelu(x):
    return 0.5 * x * (1.0 + jnp.tanh(0.7978845608028654 * x * (1.0 + 0.044715 * (x * x))))


def pad_z(v):
    gap = jnp.zeros((v.shape[0], 64), v.dtype)
    return jnp.concatenate([gap, v, gap], axis=1)


def spread_weight(w_ref, band_ref):
    for k in range(9):
        tap = w_ref[:, k * 192 : (k + 1) * 192]
        for j in range(4):
            parts = [jnp.zeros((64, j * 64), tap.dtype)] * (j > 0) + [tap] + [jnp.zeros((64, 192 - j * 64), tap.dtype)] * (j < 3)
            band_ref[j * 64 : (j + 1) * 64, k * 384 : (k + 1) * 384] = jnp.concatenate(parts, axis=1)


def shift_rows(stack_ref, index, tile, low, high):
    stack_ref[0, index] = jnp.concatenate([low, tile[:15]], axis=0).astype(jnp.bfloat16)
    stack_ref[1, index] = tile.astype(jnp.bfloat16)
    stack_ref[2, index] = jnp.concatenate([tile[1:], high], axis=0).astype(jnp.bfloat16)


def convolve_block(gx, gy, n_gx, n_gy, latent_ref, cols_ref, hx_ref, hy_ref, hc_ref, band1_ref, band2_ref,
                   rows_ref, edge_ref, hid_ref, hcol_ref, tiles_ref):
    f32 = jnp.float32
    left, right = gx > 0, gx < n_gx - 1
    down, up = gy > 0, gy < n_gy - 1
    x_side, y_side = (left, right), (down, up)

    def halo_col(side, j):
        mid = hy_ref[side, j].astype(f32)
        low = jnp.where(left, hc_ref[0, side, j].astype(f32), 0.0)
        high = jnp.where(right, hc_ref[1, side, j].astype(f32), 0.0)
        return pad_z(jnp.where(y_side[side], jnp.concatenate([low, mid, high], axis=0), 0.0))

    def own_col(y, c):
        low = [hx_ref[0, i, y : y + 1, :].astype(f32) for i in range(2)]
        high = [hx_ref[1, i, y : y + 1, :].astype(f32) for i in range(2)]
        low = jnp.where(left, jnp.concatenate(low, axis=0), 0.0)
        high = jnp.where(right, jnp.concatenate(high, axis=0), 0.0)
        return pad_z(jnp.concatenate([low, cols_ref[c].astype(f32), high], axis=0))

    lower = [halo_col(0, 0), halo_col(0, 1), own_col(0, 0)]
    upper = [own_col(15, 3), halo_col(1, 0), halo_col(1, 1)]
    fill = jnp.zeros((6, 1152), f32)
    for dx in range(3):
        for dy in range(3):
            edge_ref[dx * 3 + dy] = jnp.concatenate(
                [lower[dy][dx : dx + 18], fill, upper[dy][dx : dx + 18], fill], axis=0).astype(jnp.bfloat16)
    for x in range(20):
        if x < 2:
            tile = jnp.where(left, hx_ref[0, x].astype(f32), 0.0)
        elif x < 18:
            tile = latent_ref[x - 2].astype(f32)
        else:
            tile = jnp.where(right, hx_ref[1, x - 18].astype(f32), 0.0)
        shift_rows(rows_ref, x, pad_z(tile), lower[1][x : x + 1], upper[1][x : x + 1])

    row24 = lax.broadcasted_iota(jnp.int32, (24, 1), 0)
    inside = jnp.logical_and(jnp.logical_or(row24 > 0, left), jnp.logical_or(row24 != 17, right))

    for b in range(4):
        lanes = slice(b * 256, b * 256 + 384)
        taps = []
        for dx in range(3):
            for dy in range(3):
                taps.append(jnp.concatenate([rows_ref[dy, dx : dx + 18, :, lanes].reshape(288, 384), edge_ref[dx * 3 + dy, :, lanes]], axis=0))
        acc = lax.dot_general(jnp.concatenate(taps, axis=1), band1_ref[...], (((1,), (1,)), ((), ())), preferred_element_type=f32)
        acc = gelu(acc)
        out = slice(b * 256, b * 256 + 256)
        hid_ref[0, :, out] = jnp.where(left, acc[:16], 0.0)
        hid_ref[1:17, :, out] = acc[16:272].reshape(16, 16, 256)
        hid_ref[17, :, out] = jnp.where(right, acc[272:288], 0.0)
        hcol_ref[0, :, out] = jnp.where(jnp.logical_and(inside, down), acc[288:312], 0.0)
        hcol_ref[1, :, out] = jnp.where(jnp.logical_and(inside, up), acc[312:336], 0.0)

    low, high = pad_z(hcol_ref[0]), pad_z(hcol_ref[1])
    for x in range(18):
        shift_rows(rows_ref, x, pad_z(hid_ref[x]), low[x : x + 1], high[x : x + 1])

    for b in range(4):
        lanes = slice(b * 256, b * 256 + 384)
        taps = [rows_ref[dy, dx : dx + 16, :, lanes].reshape(256, 384) for dx in range(3) for dy in range(3)]
        acc = lax.dot_general(jnp.concatenate(taps, axis=1), band2_ref[...], (((1,), (1,)), ((), ())), preferred_element_type=f32)
        acc = acc.reshape(16, 16, 256) + latent_ref[:, :, b * 256 : b * 256 + 256].astype(f32)
        for tx in range(4):
            for ty in range(4):
                tile = [acc[tx * 4 + i, ty * 4 : ty * 4 + 4] for i in range(4)]
                tiles_ref[(tx * 4 + ty) * 4 + b] = jnp.concatenate(tile, axis=0).astype(jnp.bfloat16)


MESH = pl.DeviceIdType.MESH
PB = 512
CHUNKS = 4


def window_kernel(latent, cols, corner, touch, w1, w2, w_in, w_out, anchor, frac, feat, cot,
                  pred_out, grads_out, back_out, want_out, pos_out,
                  latent_v, cols_v, w1_v, w2_v, w_in_v, w_out_v, anchor_v, frac_v, feat_v, cot_v,
                  hx_v, hy_v, hc_v, table_v, table_s,
                  band1, band2, rows, edge, hid, hcol, tiles, outgoing, received,
                  near, state, lift, mixed, wz_v, wt, wo, active, grad_pre, spread, part, pred_v,
                  load_sem, side_send, side_recv, touch_own, touch_send, touch_recv, smem_sem,
                  tile_send, tile_recv, back_own, back_send, back_recv, store_sem, *, n_gx, n_gy):
    f32, bf16 = jnp.float32, jnp.bfloat16
    count = n_gx * n_gy
    particles = anchor.shape[1]
    blocks = particles // PB
    gx, gy = lax.axis_index("gx"), lax.axis_index("gy")
    me = gx * n_gy + gy
    pos_out[0] = gx
    pos_out[1] = gy

    def device_at(k):
        index = lax.rem(me + k, count)
        return (index // n_gy, lax.rem(index, n_gy))

    loads = [pltpu.make_async_copy(a, b, load_sem.at[i]) for i, (a, b) in enumerate([
        (anchor, anchor_v), (frac, frac_v), (w_in, w_in_v), (w_out, w_out_v), (w1, w1_v), (w2, w2_v),
        (cot, cot_v), (feat, feat_v), (latent, latent_v), (cols, cols_v)])]
    for load in loads:
        load.start()

    barrier = pltpu.get_barrier_semaphore()

    def greet(k, carry):
        pl.semaphore_signal(barrier, inc=1, device_id=device_at(k), device_id_type=MESH)
        return carry

    lax.fori_loop(1, count, greet, 0)

    for load in loads[:6]:
        load.wait()
    wt[...] = w_in_v[...].T
    wide = w_out_v[...].astype(f32).T
    wo[...] = jnp.concatenate([wide, wide, wide, jnp.zeros_like(wide)], axis=1).astype(bf16)
    spread_weight(w1_v, band1)
    spread_weight(w2_v, band2)

    def weigh(i, carry):
        span = pl.ds(pl.multiple_of(i * PB, PB), PB)
        place = anchor_v[:, span]
        offset = frac_v[:, span]
        cell = lax.broadcasted_iota(jnp.int32, (16, PB), 0)
        off_x = (cell >> 2) - ((place >> 4) & 3)
        off_y = (cell & 3) - ((place >> 2) & 3)
        off_z = lax.broadcasted_iota(jnp.int32, (4, PB), 0) - (place & 3)
        dist_x = offset[0:1] - off_x.astype(f32)
        dist_y = offset[1:2] - off_y.astype(f32)
        dist_z = offset[2:3] - off_z.astype(f32)
        beside = jnp.logical_and(jnp.abs(off_x) <= 1, jnp.abs(off_y) <= 1)
        kxy = jnp.where(beside, jnp.exp(-(dist_x * dist_x + dist_y * dist_y)), 0.0)
        kz = jnp.where(jnp.abs(off_z) <= 1, jnp.exp(-(dist_z * dist_z)), 0.0)
        wxy = (kxy / jnp.sum(kxy, axis=0, keepdims=True)).astype(bf16)
        wz_v[:, span] = kz / jnp.sum(kz, axis=0, keepdims=True)
        distance = (me + count - (place >> 6)) & (count - 1)
        distance = jnp.broadcast_to(distance.astype(f32), (16, PB)).astype(bf16)
        zero = jnp.zeros_like(wxy)
        for k in range(count):
            near[k * 16 : (k + 1) * 16, span] = jnp.where(distance == bf16(k), wxy, zero)
        return carry

    lax.fori_loop(0, blocks, weigh, 0)

    pl.semaphore_wait(barrier, count - 1)
    low_x, high_x = lax.rem(gx + n_gx - 1, n_gx), lax.rem(gx + 1, n_gx)
    low_y, high_y = lax.rem(gy + n_gy - 1, n_gy), lax.rem(gy + 1, n_gy)
    moves = [
        (latent.at[pl.ds(0, 2)], hx_v.at[1], (low_x, gy)),
        (latent.at[pl.ds(14, 2)], hx_v.at[0], (high_x, gy)),
        (cols.at[pl.ds(0, 2)], hy_v.at[1], (gx, low_y)),
        (cols.at[pl.ds(2, 2)], hy_v.at[0], (gx, high_y)),
    ]
    for i, near_x in enumerate((low_x, high_x)):
        for j, near_y in enumerate((low_y, high_y)):
            moves.append((corner.at[i, j], hc_v.at[1 - i, 1 - j], (near_x, near_y)))
    sides = [pltpu.make_async_remote_copy(src_ref=a, dst_ref=b, send_sem=side_send.at[m], recv_sem=side_recv.at[m],
                                          device_id=device, device_id_type=MESH) for m, (a, b, device) in enumerate(moves)]
    for copy in sides:
        copy.start()
    own_touch = pltpu.make_async_copy(touch.at[0], table_v.at[me], touch_own)
    own_touch.start()

    def tell(k, carry):
        pltpu.make_async_remote_copy(src_ref=touch.at[0], dst_ref=table_v.at[me], send_sem=touch_send, recv_sem=touch_recv,
                                     device_id=device_at(k), device_id_type=MESH).start()
        return carry

    lax.fori_loop(1, count, tell, 0)

    for load in loads[6:]:
        load.wait()

    def prepare(i, carry):
        span = pl.ds(pl.multiple_of(i * PB, PB), PB)
        state[:, span] = jnp.dot(wt[:, 64:], feat_v[:, span], preferred_element_type=f32)
        given = cot_v[:, span]
        high = given.astype(bf16).astype(f32)
        rest = given - high
        mid = rest.astype(bf16).astype(f32)
        pieces = jnp.concatenate([high, mid, rest - mid, jnp.zeros_like(high)], axis=0).astype(bf16)
        lift[:, span] = jnp.dot(wo[...], pieces, preferred_element_type=f32)
        return carry

    lax.fori_loop(0, blocks, prepare, 0)

    for copy in sides:
        copy.wait()
    convolve_block(gx, gy, n_gx, n_gy, latent_v, cols_v, hx_v, hy_v, hc_v, band1, band2, rows, edge, hid, hcol, tiles)

    own_touch.wait()
    others = table_v.at[pl.ds(0, count - 1)]
    pltpu.make_async_copy(others, others, touch_recv).wait()
    pltpu.make_async_copy(others, others, touch_send).wait()
    to_smem = pltpu.make_async_copy(table_v, table_s, smem_sem)
    to_smem.start()
    to_smem.wait()

    def pick(k, carry):
        wanted = table_s[lax.rem(me + k, count), 0, me]
        want_out[k] = wanted
        tile = tiles[jnp.maximum(wanted, 0)]
        outgoing[k] = jnp.where(wanted >= 0, tile, jnp.zeros_like(tile))
        return carry

    lax.fori_loop(0, count, pick, 0)
    part_slots = count // CHUNKS

    def send_tile(k, carry):
        pltpu.make_async_remote_copy(src_ref=outgoing.at[k], dst_ref=received.at[k], send_sem=tile_send, recv_sem=tile_recv.at[k // part_slots],
                                     device_id=device_at(k), device_id_type=MESH).start()
        return carry

    lax.fori_loop(1, count, send_tile, 0)
    received[0] = outgoing[0]

    for q in range(CHUNKS):
        first = 1 if q == 0 else q * part_slots
        arriving = received.at[pl.ds(first, (q + 1) * part_slots - first)]
        pltpu.make_async_copy(arriving, arriving, tile_recv.at[q]).wait()
        turned = received[q * part_slots : (q + 1) * part_slots].reshape(part_slots * 16, 256).T

        def gather(i, carry):
            span = pl.ds(pl.multiple_of(i * PB, PB), PB)
            value = jnp.dot(turned, near[q * part_slots * 16 : (q + 1) * part_slots * 16, span], preferred_element_type=f32)
            mixed[:, span] = value if q == 0 else mixed[:, span] + value
            return carry

        lax.fori_loop(0, blocks, gather, 0)

    def hidden(i, carry):
        span = pl.ds(pl.multiple_of(i * PB, PB), PB)
        wz = wz_v[:, span]
        sampled = mixed[0:64, span] * wz[0:1]
        for z in range(1, 4):
            sampled = sampled + mixed[z * 64 : z * 64 + 64, span] * wz[z : z + 1]
        preact = state[:, span] + jnp.dot(wt[:, :64], sampled.astype(bf16), preferred_element_type=f32)
        value, slope = gelu_pair(preact)
        active[:, span] = value.astype(bf16)
        grad = (lift[:, span] * slope).astype(bf16)
        grad_pre[:, span] = grad
        back = jnp.dot(w_in_v[0:64, :], grad, preferred_element_type=f32)
        for z in range(4):
            spread[z * 64 : z * 64 + 64, span] = (back * wz[z : z + 1]).astype(bf16)
        return carry

    lax.fori_loop(0, blocks, hidden, 0)

    def scatter(q, carry):
        band = pl.ds(pl.multiple_of(q * part_slots * 16, part_slots * 16), part_slots * 16)
        value = lax.dot_general(near[band, :], spread[...], (((1,), (1,)), ((), ())), preferred_element_type=f32)
        part[pl.ds(q * part_slots, part_slots)] = value.astype(bf16).reshape(part_slots, 16, 256)

        def send_back(j, inner):
            k = q * part_slots + j
            pltpu.make_async_remote_copy(src_ref=part.at[k], dst_ref=back_out.at[k], send_sem=back_send, recv_sem=back_recv,
                                         device_id=device_at(count - k), device_id_type=MESH).start()
            return inner

        return lax.fori_loop(jnp.where(q == 0, 1, 0), part_slots, send_back, carry)

    lax.fori_loop(0, CHUNKS, scatter, 0)
    own_back = pltpu.make_async_copy(part.at[0], back_out.at[0], back_own)
    own_back.start()

    def finish(i, carry):
        span = pl.ds(pl.multiple_of(i * PB, PB), PB)
        pred_v[:, span] = jnp.dot(w_out_v[...], active[:, span], preferred_element_type=f32)
        feat_v[:, span] = jnp.dot(w_in_v[64:, :], grad_pre[:, span], preferred_element_type=f32).astype(bf16)
        return carry

    lax.fori_loop(0, blocks, finish, 0)
    stores = [pltpu.make_async_copy(pred_v, pred_out, store_sem.at[0]), pltpu.make_async_copy(feat_v, grads_out, store_sem.at[1])]
    for store in stores:
        store.start()
    sent = outgoing.at[pl.ds(0, count - 1)]
    pltpu.make_async_copy(sent, sent, tile_send).wait()
    sent = part.at[pl.ds(0, count - 1)]
    pltpu.make_async_copy(sent, sent, back_send).wait()
    own_back.wait()
    for store in stores:
        store.wait()
    landed = back_out.at[pl.ds(0, count - 1)]
    pltpu.make_async_copy(landed, landed, back_recv).wait()


def window(latent, cols, corner, touch, w1, w2, w_in, w_out, anchor, frac, feat, cot, n_gx, n_gy):
    hbm = pl.BlockSpec(memory_space=pl.ANY)
    smem = pl.BlockSpec(memory_space=pltpu.SMEM)
    bf, f32, i32 = jnp.bfloat16, jnp.float32, jnp.int32
    count = n_gx * n_gy
    particles = anchor.shape[1]
    dma = pltpu.SemaphoreType.DMA
    vmem = lambda a: pltpu.VMEM(a.shape, a.dtype)
    shaped = jax.ShapeDtypeStruct
    return pl.pallas_call(
        functools.partial(window_kernel, n_gx=n_gx, n_gy=n_gy),
        in_specs=[hbm] * 12,
        out_specs=[hbm, hbm, hbm, smem, smem],
        out_shape=[shaped((4, particles), f32), shaped((256, particles), bf), shaped((count, 16, 256), bf), shaped((count,), i32), shaped((2,), i32)],
        scratch_shapes=[
            vmem(latent), vmem(cols), vmem(w1), vmem(w2), vmem(w_in), vmem(w_out), vmem(anchor), vmem(frac), vmem(feat), vmem(cot),
            pltpu.VMEM((2, 2, 16, 1024), bf), pltpu.VMEM((2, 2, 16, 1024), bf), pltpu.VMEM((2, 2, 2, 2, 1024), bf),
            pltpu.VMEM((count, 1, count), i32), pltpu.SMEM((count, 1, count), i32),
            pltpu.VMEM((256, 3456), bf), pltpu.VMEM((256, 3456), bf), pltpu.VMEM((3, 20, 16, 1152), bf), pltpu.VMEM((9, 48, 1152), bf),
            pltpu.VMEM((18, 16, 1024), f32), pltpu.VMEM((2, 24, 1024), f32), pltpu.VMEM((64, 16, 256), bf),
            pltpu.VMEM((count, 16, 256), bf), pltpu.VMEM((count, 16, 256), bf),
            pltpu.VMEM((count * 16, particles), bf), pltpu.VMEM((256, particles), f32), pltpu.VMEM((256, particles), f32),
            pltpu.VMEM((256, particles), f32), pltpu.VMEM((4, particles), f32), pltpu.VMEM((256, 320), bf), pltpu.VMEM((256, 16), bf),
            pltpu.VMEM((256, particles), bf), pltpu.VMEM((256, particles), bf), pltpu.VMEM((256, particles), bf),
            pltpu.VMEM((count, 16, 256), bf), pltpu.VMEM((4, particles), f32),
            dma((10,)), dma((8,)), dma((8,)), dma(()), dma(()), dma(()), dma(()),
            dma(()), dma((CHUNKS,)), dma(()), dma(()), dma(()), dma((2,)),
        ],
        compiler_params=pltpu.CompilerParams(collective_id=0, has_side_effects=True, vmem_limit_bytes=62 << 20),
        name="window",
    )(latent, cols, corner, touch, w1, w2, w_in, w_out, anchor, frac, feat, cot)


def collect_kernel(want_ref, back_ref, out_ref, sum_ref):
    sum_ref[...] = jnp.zeros_like(sum_ref)

    def add(k, carry):
        wanted = want_ref[k]
        sum_ref[jnp.where(wanted >= 0, wanted, 64)] += back_ref[k].astype(jnp.float32)
        return carry

    lax.fori_loop(0, back_ref.shape[0], add, 0, unroll=8)
    for tx in range(4):
        for ty in range(4):
            for tz in range(4):
                tile = sum_ref[(tx * 4 + ty) * 4 + tz]
                for i in range(4):
                    out_ref[tx * 4 + i, ty * 4 : ty * 4 + 4, tz * 256 : tz * 256 + 256] = tile[i * 4 : i * 4 + 4]


def collect(want, back):
    return pl.pallas_call(
        collect_kernel,
        in_specs=[pl.BlockSpec(memory_space=pltpu.SMEM), pl.BlockSpec(memory_space=pltpu.VMEM)],
        out_specs=pl.BlockSpec(memory_space=pltpu.VMEM),
        out_shape=jax.ShapeDtypeStruct((16, 16, 1024), jnp.float32),
        scratch_shapes=[pltpu.VMEM((65, 16, 256), jnp.float32)],
        compiler_params=pltpu.CompilerParams(vmem_limit_bytes=32 << 20),
        name="collect",
    )(want, back)


def make_body(n_gx, n_gy):
    def body(latent, conv_first, conv_second, w_in, w_out, touch, anchor, frac, pfeat, cotangent):
        cols = jnp.stack([latent[:, 0], latent[:, 1], latent[:, 14], latent[:, 15]])
        corner = jnp.stack([jnp.stack([cols[2 * j : 2 * j + 2, 14 * i : 14 * i + 2] for j in range(2)]) for i in range(2)])
        predicted, feature_grads, back, want, _ = window(
            latent, cols, corner, touch.reshape(1, 1, -1), conv_first, conv_second, w_in, w_out,
            anchor.reshape(1, -1), frac, pfeat, cotangent, n_gx, n_gy)
        return (predicted, feature_grads, collect(want, back))

    return body


def solution(mesh):
    rows = P(("gx", "gy"), None)
    cols = P(None, ("gx", "gy"))
    grid = P("gx", "gy", None)
    return jax.shard_map(
        make_body(mesh.shape["gx"], mesh.shape["gy"]),
        mesh=mesh,
        in_specs=(grid, P(), P(), P(), P(), rows, P(("gx", "gy")), cols, cols, cols),
        out_specs=(cols, cols, grid),
        check_vma=False,
    )
```

time: 107 us -> 84.4 us (0.79)
  the two profiles are of different devices: /device:TPU:1 before, /device:TPU:0 now
where the time goes in v2:
time: 84.4 us; the launch traced here: 84.2 us
  Pallas kernels  75.8 us (90%)
  local copies, waits for them, and re-layouts  6.24 us (7%)
  other arithmetic  1.43 us (2%)
    pallas_call x1, Pallas kernels, window(): pl.pallas_call(functools.partial(window_kernel, n_gx=n_gx, n_gy=n_gy), in...  73.6 us
    unnamed x8, local copies, waits for them, and re-layouts  4.64 us
    pallas_call x1, Pallas kernels, collect(): pl.pallas_call(collect_kernel, in_specs=[pl.BlockSpec(memory_space=pltpu....  2.25 us

profile of v2, /device:TPU:0, one launch (start us, length us, event | category | flops | bytes accessed | tf_op | source)
XLA Modules:
  0.0 84.2 jit_solution(9551628757670316847)
XLA Ops:
  0.6 1.6 %fusion.2 = (bf16[16,1,1024]{2,1,0:T(2,128)(2,1)S(1)}, bf16[16,1,1024]{2,1,0:T(2,128)(2,1)S(1)}, bf16[16,1,1024]{2,1,0:T(2,128)(2,1)S(1)}, bf16[16,1,1024]{2,1,0:T(2,128)(2,1)S(1)}) fusion(bf16[16,16,1024]{2,1,0:T(8,128)(2,1)} %latent.1), kind=kLoop, calls=%fused_computation.14 | loop fusion | bytes 262144 | tf_op jit(solution)/shard_map/slice | solution.py:393
  2.3 0.7 pad_maximum_fusion.cols
  3.0 0.7 pad_maximum_fusion.1.corner
  3.7 73.6 %window.1 = (f32[4,4096]{1,0:T(4,128)}, bf16[256,4096]{1,0:T(8,128)(2,1)}, bf16[128,16,256]{2,1,0:T(8,128)(2,1)}, s32[128]{0:T(128)}, s32[2]{0:T(128)}) custom-call(bf16[16,16,1024]{2,1,0:T(8,128)(2,1)} %latent.1, bf16[4,16,1024]{2,1,0:T(8,128)(2,1)} %pad_maximum_fusion.cols, bf16[2,2,2,2,1024]{4,3,2,1,0:T(2,128)(2,1)} %pad_maximum_fusion.1.corner, ...), custom_call_target="tpu_custom_call" | custom-call | tf_op jit(solution)/shard_map/window/pallas_call | solution.py:338
  77.3 0.0 copy-start
  77.3 1.2 %copy-done = bf16[128,16,256]{2,1,0:T(8,128)(2,1)S(1)} copy-done((bf16[128,16,256]{2,1,0:T(8,128)(2,1)S(1)}, bf16[128,16,256]{2,1,0:T(8,128)(2,1)}, u32[]{:S(2)}) %copy-start) | copy-done | bytes 1048600
  78.5 0.0 copy-start.1
  78.5 0.6 copy-done.1
  79.1 0.0 copy-start.2
  79.1 2.3 %collect.1 = f32[16,16,1024]{2,1,0:T(8,128)} custom-call(s32[128]{0:T(128)S(1)} %copy-done.1, bf16[128,16,256]{2,1,0:T(8,128)(2,1)S(1)} %copy-done), custom_call_target="tpu_custom_call" | custom-call | tf_op jit(solution)/shard_map/collect/pallas_call | solution.py:380
  81.4 1.5 %copy.27 = f32[4,4096]{1,0:T(4,128)} copy(f32[4,4096]{1,0:T(4,128)} %get-tuple-element.26) | data formatting | bytes 131072
  82.8 0.0 copy-done.2
  82.8 1.3 %copy.28 = bf16[256,4096]{1,0:T(8,128)(2,1)} copy(bf16[256,4096]{1,0:T(8,128)(2,1)S(1)} %copy-done.2) | data formatting | bytes 4194304
  (6 shorter events, 0.1 us)
Async XLA Ops:
  77.3 1.2 %copy-start = (bf16[128,16,256]{2,1,0:T(8,128)(2,1)S(1)}, bf16[128,16,256]{2,1,0:T(8,128)(2,1)}, u32[]{:S(2)}) copy-start(bf16[128,16,256]{2,1,0:T(8,128)(2,1)} %get-tuple-element.10.back_ref) | copy-start | bytes 3145732
  78.5 0.6 copy-start.1
  79.1 3.7 %copy-start.2 = (bf16[256,4096]{1,0:T(8,128)(2,1)S(1)}, bf16[256,4096]{1,0:T(8,128)(2,1)}, u32[]{:S(2)}) copy-start(bf16[256,4096]{1,0:T(8,128)(2,1)} %get-tuple-element.27) | copy-start | bytes 6291460

commit v3 on v2

--- a/solution.py
+++ b/solution.py
@@ -42,8 +42,7 @@
     stack_ref[2, index] = jnp.concatenate([tile[1:], high], axis=0).astype(jnp.bfloat16)
 
 
-def convolve_block(gx, gy, n_gx, n_gy, latent_ref, cols_ref, hx_ref, hy_ref, hc_ref, band1_ref, band2_ref,
-                   rows_ref, edge_ref, hid_ref, hcol_ref, tiles_ref):
+def convolve_first(gx, gy, n_gx, n_gy, latent_ref, cols_ref, hx_ref, hy_ref, hc_ref, band1_ref, rows_ref, edge_ref, hid_ref, hcol_ref):
     f32 = jnp.float32
     left, right = gx > 0, gx < n_gx - 1
     down, up = gy > 0, gy < n_gy - 1
@@ -96,6 +95,9 @@
         hcol_ref[0, :, out] = jnp.where(jnp.logical_and(inside, down), acc[288:312], 0.0)
         hcol_ref[1, :, out] = jnp.where(jnp.logical_and(inside, up), acc[312:336], 0.0)
 
+
+def convolve_second(latent_ref, band2_ref, rows_ref, hid_ref, hcol_ref, tiles_ref):
+    f32 = jnp.float32
     low, high = pad_z(hcol_ref[0]), pad_z(hcol_ref[1])
     for x in range(18):
         shift_rows(rows_ref, x, pad_z(hid_ref[x]), low[x : x + 1], high[x : x + 1])
@@ -112,13 +114,14 @@
 
 
 MESH = pl.DeviceIdType.MESH
-PB = 512
-CHUNKS = 4
-
-
-def window_kernel(latent, cols, corner, touch, w1, w2, w_in, w_out, anchor, frac, feat, cot,
-                  pred_out, grads_out, back_out, want_out, pos_out,
-                  latent_v, cols_v, w1_v, w2_v, w_in_v, w_out_v, anchor_v, frac_v, feat_v, cot_v,
+PB = 1024
+CHUNKS = 8
+GROUPS = ((0, 32), (32, 64), (64, 96), (96, 128))
+
+
+def window_kernel(latent, touch, w1, w2, w_in, w_out, anchor, frac, feat, cot,
+                  pred_out, grads_out, back_out, want_out,
+                  latent_v, cols_v, corner_v, w1_v, w2_v, w_in_v, w_out_v, anchor_v, frac_v, feat_v, cot_v,
                   hx_v, hy_v, hc_v, table_v, table_s,
                   band1, band2, rows, edge, hid, hcol, tiles, outgoing, received,
                   near, state, lift, mixed, wz_v, wt, wo, active, grad_pre, spread, part, pred_v,
@@ -130,34 +133,118 @@
     blocks = particles // PB
     gx, gy = lax.axis_index("gx"), lax.axis_index("gy")
     me = gx * n_gy + gy
-    pos_out[0] = gx
-    pos_out[1] = gy
 
     def device_at(k):
         index = lax.rem(me + k, count)
         return (index // n_gy, lax.rem(index, n_gy))
 
     loads = [pltpu.make_async_copy(a, b, load_sem.at[i]) for i, (a, b) in enumerate([
-        (anchor, anchor_v), (frac, frac_v), (w_in, w_in_v), (w_out, w_out_v), (w1, w1_v), (w2, w2_v),
-        (cot, cot_v), (feat, feat_v), (latent, latent_v), (cols, cols_v)])]
+        (latent, latent_v), (w1, w1_v), (w2, w2_v), (w_in, w_in_v), (w_out, w_out_v), (cot, cot_v), (feat, feat_v),
+        (anchor, anchor_v), (frac, frac_v)])]
     for load in loads:
         load.start()
-
+    own_touch = pltpu.make_async_copy(touch.at[0], table_v.at[me], touch_own)
+    own_touch.start()
+
+    along_y = [(gx, lax.rem(gy + j, n_gy)) for j in range(1, n_gy)]
+    along_x = [(lax.rem(gx + i, n_gx), gy) for i in range(1, n_gx)]
+    low_x, high_x = lax.rem(gx + n_gx - 1, n_gx), lax.rem(gx + 1, n_gx)
+    low_y, high_y = lax.rem(gy + n_gy - 1, n_gy), lax.rem(gy + 1, n_gy)
+    diagonal = [(near_x, near_y) for near_x in (low_x, high_x) for near_y in (low_y, high_y)]
     barrier = pltpu.get_barrier_semaphore()
-
-    def greet(k, carry):
-        pl.semaphore_signal(barrier, inc=1, device_id=device_at(k), device_id_type=MESH)
-        return carry
-
-    lax.fori_loop(1, count, greet, 0)
-
-    for load in loads[:6]:
+    greeted = diagonal + along_x + along_y
+    for device in greeted:
+        pl.semaphore_signal(barrier, inc=1, device_id=device, device_id_type=MESH)
+
+    loads[0].wait()
+    for c, y in enumerate((0, 1, 14, 15)):
+        column = jnp.concatenate([latent_v[x, y : y + 1, :].astype(f32) for x in range(16)], axis=0)
+        cols_v[c] = column.astype(bf16)
+        for i in range(2):
+            corner_v[i, c // 2, c % 2] = column[14 * i : 14 * i + 2].astype(bf16)
+
+    pl.semaphore_wait(barrier, len(greeted))
+    moves = [
+        (latent_v.at[pl.ds(0, 2)], hx_v.at[1], (low_x, gy)),
+        (latent_v.at[pl.ds(14, 2)], hx_v.at[0], (high_x, gy)),
+        (cols_v.at[pl.ds(0, 2)], hy_v.at[1], (gx, low_y)),
+        (cols_v.at[pl.ds(2, 2)], hy_v.at[0], (gx, high_y)),
+    ]
+    for i, near_x in enumerate((low_x, high_x)):
+        for j, near_y in enumerate((low_y, high_y)):
+            moves.append((corner_v.at[i, j], hc_v.at[1 - i, 1 - j], (near_x, near_y)))
+    sides = [pltpu.make_async_remote_copy(src_ref=a, dst_ref=b, send_sem=side_send.at[m], recv_sem=side_recv.at[m],
+                                          device_id=device, device_id_type=MESH) for m, (a, b, device) in enumerate(moves)]
+    for copy in sides:
+        copy.start()
+    for device in along_y:
+        pltpu.make_async_remote_copy(src_ref=touch.at[0], dst_ref=table_v.at[me], send_sem=touch_send.at[0], recv_sem=touch_recv.at[0],
+                                     device_id=device, device_id_type=MESH).start()
+
+    for load in loads[1:7]:
         load.wait()
     wt[...] = w_in_v[...].T
     wide = w_out_v[...].astype(f32).T
     wo[...] = jnp.concatenate([wide, wide, wide, jnp.zeros_like(wide)], axis=1).astype(bf16)
     spread_weight(w1_v, band1)
     spread_weight(w2_v, band2)
+
+    def prepare(i, carry):
+        span = pl.ds(pl.multiple_of(i * PB, PB), PB)
+        state[:, span] = jnp.dot(wt[:, 64:], feat_v[:, span], preferred_element_type=f32)
+        given = cot_v[:, span]
+        high = given.astype(bf16).astype(f32)
+        rest = given - high
+        mid = rest.astype(bf16).astype(f32)
+        pieces = jnp.concatenate([high, mid, rest - mid, jnp.zeros_like(high)], axis=0).astype(bf16)
+        lift[:, span] = jnp.dot(wo[...], pieces, preferred_element_type=f32)
+        return carry
+
+    lax.fori_loop(0, blocks, prepare, 0)
+
+    for copy in sides:
+        copy.wait()
+    own_touch.wait()
+    line = table_v.at[pl.ds(0, n_gy - 1)]
+    pltpu.make_async_copy(line, line, touch_recv.at[0]).wait()
+    mine = table_v.at[pl.ds(gx * n_gy, n_gy)]
+    for device in along_x:
+        pltpu.make_async_remote_copy(src_ref=mine, dst_ref=mine, send_sem=touch_send.at[1], recv_sem=touch_recv.at[1],
+                                     device_id=device, device_id_type=MESH).start()
+    convolve_first(gx, gy, n_gx, n_gy, latent_v, cols_v, hx_v, hy_v, hc_v, band1, rows, edge, hid, hcol)
+    plane = table_v.at[pl.ds(0, count - n_gy)]
+    pltpu.make_async_copy(plane, plane, touch_recv.at[1]).wait()
+    to_smem = pltpu.make_async_copy(table_v, table_s, smem_sem)
+    to_smem.start()
+    convolve_second(latent_v, band2, rows, hid, hcol, tiles)
+    to_smem.wait()
+    pltpu.make_async_copy(line, line, touch_send.at[0]).wait()
+    pltpu.make_async_copy(plane, plane, touch_send.at[1]).wait()
+
+    def pick(k, carry):
+        wanted = table_s[lax.rem(me + k, count), 0, me]
+        want_out[k] = wanted
+        tile = tiles[jnp.maximum(wanted, 0)]
+        outgoing[k] = jnp.where(wanted >= 0, tile, jnp.zeros_like(tile))
+        return carry
+
+    lax.fori_loop(0, count, pick, 0, unroll=8)
+    part_slots = count // CHUNKS
+
+    def wait_for(ref, sem):
+        pltpu.make_async_copy(ref, ref, sem).wait()
+
+    for g, (first, last) in enumerate(GROUPS):
+
+        def send_tile(k, carry):
+            pltpu.make_async_remote_copy(src_ref=outgoing.at[k], dst_ref=received.at[k], send_sem=tile_send, recv_sem=tile_recv.at[g],
+                                         device_id=device_at(k), device_id_type=MESH).start()
+            return carry
+
+        lax.fori_loop(max(1, first), last, send_tile, 0)
+    received[0] = outgoing[0]
+    for load in loads[7:]:
+        load.wait()
 
     def weigh(i, carry):
         span = pl.ds(pl.multiple_of(i * PB, PB), PB)
@@ -184,91 +271,14 @@
 
     lax.fori_loop(0, blocks, weigh, 0)
 
-    pl.semaphore_wait(barrier, count - 1)
-    low_x, high_x = lax.rem(gx + n_gx - 1, n_gx), lax.rem(gx + 1, n_gx)
-    low_y, high_y = lax.rem(gy + n_gy - 1, n_gy), lax.rem(gy + 1, n_gy)
-    moves = [
-        (latent.at[pl.ds(0, 2)], hx_v.at[1], (low_x, gy)),
-        (latent.at[pl.ds(14, 2)], hx_v.at[0], (high_x, gy)),
-        (cols.at[pl.ds(0, 2)], hy_v.at[1], (gx, low_y)),
-        (cols.at[pl.ds(2, 2)], hy_v.at[0], (gx, high_y)),
-    ]
-    for i, near_x in enumerate((low_x, high_x)):
-        for j, near_y in enumerate((low_y, high_y)):
-            moves.append((corner.at[i, j], hc_v.at[1 - i, 1 - j], (near_x, near_y)))
-    sides = [pltpu.make_async_remote_copy(src_ref=a, dst_ref=b, send_sem=side_send.at[m], recv_sem=side_recv.at[m],
-                                          device_id=device, device_id_type=MESH) for m, (a, b, device) in enumerate(moves)]
-    for copy in sides:
-        copy.start()
-    own_touch = pltpu.make_async_copy(touch.at[0], table_v.at[me], touch_own)
-    own_touch.start()
-
-    def tell(k, carry):
-        pltpu.make_async_remote_copy(src_ref=touch.at[0], dst_ref=table_v.at[me], send_sem=touch_send, recv_sem=touch_recv,
-                                     device_id=device_at(k), device_id_type=MESH).start()
-        return carry
-
-    lax.fori_loop(1, count, tell, 0)
-
-    for load in loads[6:]:
-        load.wait()
-
-    def prepare(i, carry):
-        span = pl.ds(pl.multiple_of(i * PB, PB), PB)
-        state[:, span] = jnp.dot(wt[:, 64:], feat_v[:, span], preferred_element_type=f32)
-        given = cot_v[:, span]
-        high = given.astype(bf16).astype(f32)
-        rest = given - high
-        mid = rest.astype(bf16).astype(f32)
-        pieces = jnp.concatenate([high, mid, rest - mid, jnp.zeros_like(high)], axis=0).astype(bf16)
-        lift[:, span] = jnp.dot(wo[...], pieces, preferred_element_type=f32)
-        return carry
-
-    lax.fori_loop(0, blocks, prepare, 0)
-
-    for copy in sides:
-        copy.wait()
-    convolve_block(gx, gy, n_gx, n_gy, latent_v, cols_v, hx_v, hy_v, hc_v, band1, band2, rows, edge, hid, hcol, tiles)
-
-    own_touch.wait()
-    others = table_v.at[pl.ds(0, count - 1)]
-    pltpu.make_async_copy(others, others, touch_recv).wait()
-    pltpu.make_async_copy(others, others, touch_send).wait()
-    to_smem = pltpu.make_async_copy(table_v, table_s, smem_sem)
-    to_smem.start()
-    to_smem.wait()
-
-    def pick(k, carry):
-        wanted = table_s[lax.rem(me + k, count), 0, me]
-        want_out[k] = wanted
-        tile = tiles[jnp.maximum(wanted, 0)]
-        outgoing[k] = jnp.where(wanted >= 0, tile, jnp.zeros_like(tile))
-        return carry
-
-    lax.fori_loop(0, count, pick, 0)
-    part_slots = count // CHUNKS
-
-    def send_tile(k, carry):
-        pltpu.make_async_remote_copy(src_ref=outgoing.at[k], dst_ref=received.at[k], send_sem=tile_send, recv_sem=tile_recv.at[k // part_slots],
-                                     device_id=device_at(k), device_id_type=MESH).start()
-        return carry
-
-    lax.fori_loop(1, count, send_tile, 0)
-    received[0] = outgoing[0]
-
-    for q in range(CHUNKS):
-        first = 1 if q == 0 else q * part_slots
-        arriving = received.at[pl.ds(first, (q + 1) * part_slots - first)]
-        pltpu.make_async_copy(arriving, arriving, tile_recv.at[q]).wait()
-        turned = received[q * part_slots : (q + 1) * part_slots].reshape(part_slots * 16, 256).T
-
-        def gather(i, carry):
-            span = pl.ds(pl.multiple_of(i * PB, PB), PB)
-            value = jnp.dot(turned, near[q * part_slots * 16 : (q + 1) * part_slots * 16, span], preferred_element_type=f32)
-            mixed[:, span] = value if q == 0 else mixed[:, span] + value
-            return carry
-
-        lax.fori_loop(0, blocks, gather, 0)
+    for g, (first, last) in enumerate(GROUPS):
+        arrived = max(1, first)
+        wait_for(received.at[pl.ds(arrived, last - arrived)], tile_recv.at[g])
+        turned = received[first:last].reshape((last - first) * 16, 256).T
+        for i in range(blocks):
+            span = slice(i * PB, (i + 1) * PB)
+            value = jnp.dot(turned, near[first * 16 : last * 16, span], preferred_element_type=f32)
+            mixed[:, span] = value if g == 0 else mixed[:, span] + value
 
     def hidden(i, carry):
         span = pl.ds(pl.multiple_of(i * PB, PB), PB)
@@ -315,8 +325,7 @@
     stores = [pltpu.make_async_copy(pred_v, pred_out, store_sem.at[0]), pltpu.make_async_copy(feat_v, grads_out, store_sem.at[1])]
     for store in stores:
         store.start()
-    sent = outgoing.at[pl.ds(0, count - 1)]
-    pltpu.make_async_copy(sent, sent, tile_send).wait()
+    wait_for(outgoing.at[pl.ds(0, count - 1)], tile_send)
     sent = part.at[pl.ds(0, count - 1)]
     pltpu.make_async_copy(sent, sent, back_send).wait()
     own_back.wait()
@@ -326,8 +335,8 @@
     pltpu.make_async_copy(landed, landed, back_recv).wait()
 
 
-def window(latent, cols, corner, touch, w1, w2, w_in, w_out, anchor, frac, feat, cot, n_gx, n_gy):
-    hbm = pl.BlockSpec(memory_space=pl.ANY)
+def window(latent, touch, w1, w2, w_in, w_out, anchor, frac, feat, cot, n_gx, n_gy):
+    hbm = pl.BlockSpec(memory_space=pltpu.HBM)
     smem = pl.BlockSpec(memory_space=pltpu.SMEM)
     bf, f32, i32 = jnp.bfloat16, jnp.float32, jnp.int32
     count = n_gx * n_gy
@@ -337,11 +346,11 @@
     shaped = jax.ShapeDtypeStruct
     return pl.pallas_call(
         functools.partial(window_kernel, n_gx=n_gx, n_gy=n_gy),
-        in_specs=[hbm] * 12,
-        out_specs=[hbm, hbm, hbm, smem, smem],
-        out_shape=[shaped((4, particles), f32), shaped((256, particles), bf), shaped((count, 16, 256), bf), shaped((count,), i32), shaped((2,), i32)],
+        in_specs=[hbm] * 10,
+        out_specs=[hbm, hbm, hbm, smem],
+        out_shape=[shaped((4, particles), f32), shaped((256, particles), bf), shaped((count, 16, 256), bf), shaped((count,), i32)],
         scratch_shapes=[
-            vmem(latent), vmem(cols), vmem(w1), vmem(w2), vmem(w_in), vmem(w_out), vmem(anchor), vmem(frac), vmem(feat), vmem(cot),
+            vmem(latent), pltpu.VMEM((4, 16, 1024), bf), pltpu.VMEM((2, 2, 2, 2, 1024), bf), vmem(w1), vmem(w2), vmem(w_in), vmem(w_out), vmem(anchor), vmem(frac), vmem(feat), vmem(cot),
             pltpu.VMEM((2, 2, 16, 1024), bf), pltpu.VMEM((2, 2, 16, 1024), bf), pltpu.VMEM((2, 2, 2, 2, 1024), bf),
             pltpu.VMEM((count, 1, count), i32), pltpu.SMEM((count, 1, count), i32),
             pltpu.VMEM((256, 3456), bf), pltpu.VMEM((256, 3456), bf), pltpu.VMEM((3, 20, 16, 1152), bf), pltpu.VMEM((9, 48, 1152), bf),
@@ -351,51 +360,76 @@
             pltpu.VMEM((256, particles), f32), pltpu.VMEM((4, particles), f32), pltpu.VMEM((256, 320), bf), pltpu.VMEM((256, 16), bf),
             pltpu.VMEM((256, particles), bf), pltpu.VMEM((256, particles), bf), pltpu.VMEM((256, particles), bf),
             pltpu.VMEM((count, 16, 256), bf), pltpu.VMEM((4, particles), f32),
-            dma((10,)), dma((8,)), dma((8,)), dma(()), dma(()), dma(()), dma(()),
-            dma(()), dma((CHUNKS,)), dma(()), dma(()), dma(()), dma((2,)),
+            dma((9,)), dma((8,)), dma((8,)), dma(()), dma((2,)), dma((2,)), dma(()),
+            dma(()), dma((len(GROUPS),)), dma(()), dma(()), dma(()), dma((2,)),
         ],
         compiler_params=pltpu.CompilerParams(collective_id=0, has_side_effects=True, vmem_limit_bytes=62 << 20),
         name="window",
-    )(latent, cols, corner, touch, w1, w2, w_in, w_out, anchor, frac, feat, cot)
-
-
-def collect_kernel(want_ref, back_ref, out_ref, sum_ref):
-    sum_ref[...] = jnp.zeros_like(sum_ref)
-
-    def add(k, carry):
-        wanted = want_ref[k]
-        sum_ref[jnp.where(wanted >= 0, wanted, 64)] += back_ref[k].astype(jnp.float32)
-        return carry
-
-    lax.fori_loop(0, back_ref.shape[0], add, 0, unroll=8)
+    )(latent, touch, w1, w2, w_in, w_out, anchor, frac, feat, cot)
+
+
+LANES = 4
+
+
+def collect_kernel(want_ref, back, pred_in, grads_in, grid_out, pred_out, grads_out, back_v, pred_v, grads_v, grid_v, *rest):
+    sums, load_sem, store_sem = rest[:LANES], rest[LANES], rest[LANES + 1]
+    loads = [pltpu.make_async_copy(a, b, load_sem.at[i]) for i, (a, b) in enumerate([(back, back_v), (grads_in, grads_v), (pred_in, pred_v)])]
+    for load in loads:
+        load.start()
+    for sum_ref in sums:
+        sum_ref[...] = jnp.zeros_like(sum_ref)
+    loads[0].wait()
+
+    def add(j, carry):
+        for lane, sum_ref in enumerate(sums):
+            k = j * LANES + lane
+            wanted = want_ref[k]
+            sum_ref[jnp.where(wanted >= 0, wanted, 64)] += back_v[k].astype(jnp.float32)
+        return carry
+
+    lax.fori_loop(0, back_v.shape[0] // LANES, add, 0, unroll=4)
+    loads[1].wait()
+    loads[2].wait()
+    stores = [pltpu.make_async_copy(a, b, store_sem.at[i]) for i, (a, b) in enumerate([(grads_v, grads_out), (pred_v, pred_out), (grid_v, grid_out)])]
+    stores[0].start()
+    stores[1].start()
     for tx in range(4):
         for ty in range(4):
             for tz in range(4):
-                tile = sum_ref[(tx * 4 + ty) * 4 + tz]
+                t = (tx * 4 + ty) * 4 + tz
+                tile = sums[0][t]
+                for sum_ref in sums[1:]:
+                    tile = tile + sum_ref[t]
                 for i in range(4):
-                    out_ref[tx * 4 + i, ty * 4 : ty * 4 + 4, tz * 256 : tz * 256 + 256] = tile[i * 4 : i * 4 + 4]
-
-
-def collect(want, back):
+                    grid_v[tx * 4 + i, ty * 4 : ty * 4 + 4, tz * 256 : tz * 256 + 256] = tile[i * 4 : i * 4 + 4]
+    stores[2].start()
+    for store in stores:
+        store.wait()
+
+
+def collect(want, back, predicted, grads):
+    hbm = pl.BlockSpec(memory_space=pltpu.HBM)
+    shaped = jax.ShapeDtypeStruct
+    vmem = lambda a: pltpu.VMEM(a.shape, a.dtype)
+    grid = shaped((16, 16, 1024), jnp.float32)
     return pl.pallas_call(
         collect_kernel,
-        in_specs=[pl.BlockSpec(memory_space=pltpu.SMEM), pl.BlockSpec(memory_space=pltpu.VMEM)],
-        out_specs=pl.BlockSpec(memory_space=pltpu.VMEM),
-        out_shape=jax.ShapeDtypeStruct((16, 16, 1024), jnp.float32),
-        scratch_shapes=[pltpu.VMEM((65, 16, 256), jnp.float32)],
-        compiler_params=pltpu.CompilerParams(vmem_limit_bytes=32 << 20),
+        in_specs=[pl.BlockSpec(memory_space=pltpu.SMEM), hbm, hbm, hbm],
+        out_specs=[hbm, hbm, hbm],
+        out_shape=[grid, shaped(predicted.shape, predicted.dtype), shaped(grads.shape, grads.dtype)],
+        scratch_shapes=[vmem(back), vmem(predicted), vmem(grads), vmem(grid)] + [pltpu.VMEM((65, 16, 256), jnp.float32)] * LANES
+        + [pltpu.SemaphoreType.DMA((3,)), pltpu.SemaphoreType.DMA((3,))],
+        compiler_params=pltpu.CompilerParams(vmem_limit_bytes=62 << 20),
         name="collect",
-    )(want, back)
+    )(want, back, predicted, grads)
 
 
 def make_body(n_gx, n_gy):
     def body(latent, conv_first, conv_second, w_in, w_out, touch, anchor, frac, pfeat, cotangent):
-        cols = jnp.stack([latent[:, 0], latent[:, 1], latent[:, 14], latent[:, 15]])
-        corner = jnp.stack([jnp.stack([cols[2 * j : 2 * j + 2, 14 * i : 14 * i + 2] for j in range(2)]) for i in range(2)])
-        predicted, feature_grads, back, want, _ = window(
-            latent, cols, corner, touch.reshape(1, 1, -1), conv_first, conv_second, w_in, w_out,
-            anchor.reshape(1, -1), frac, pfeat, cotangent, n_gx, n_gy)
-        return (predicted, feature_grads, collect(want, back))
+        predicted, grads, back, want = window(
+            latent, touch.reshape(1, 1, -1), conv_first, conv_second, w_in, w_out, anchor.reshape(1, -1), frac, pfeat, cotangent, n_gx, n_gy)
+        grid_grad, predicted, grads = collect(want, back, predicted, grads)
+        return (predicted, grads, grid_grad)
 
     return body
 

time: 84.4 us -> 69.3 us (0.82)
  Pallas kernels: 75.8 us -> 68.6 us
  local copies, waits for them, and re-layouts: 6.24 us -> 0 us
  other arithmetic: 1.43 us -> 0 us
    pallas_call x1, Pallas kernels: 73.6 us -> 64.3 us  [window(): pl.pallas_call(functools.partial(window_kernel, n_gx=n_gx, n_gy=n_gy), in...]
    unnamed x8 -> x0, local copies, waits for them, and re-layouts: 4.64 us -> none
    pallas_call x1, Pallas kernels: 2.25 us -> 4.32 us  [collect(): pl.pallas_call(collect_kernel, in_specs=[pl.BlockSpec(memory_space=pltpu....]
    slice x1 -> x0, local copies, waits for them, and re-layouts: 1.55 us -> none  [body(): cols = jnp.stack([latent[:, 0], latent[:, 1], latent[:, 14], latent[:, 15]])]
    another operation x6 -> x0, other arithmetic: 1.43 us -> none  [the longest x3 0.72 us: body(): jnp.stack([jnp.stack([cols[2 * j:2 * j + 2, 14 * i:14 * i + 2] for j in r...]
where the time goes in v3:
time: 69.3 us; the launch traced here: 69.2 us
  Pallas kernels  68.6 us (99%)
    pallas_call x1, Pallas kernels, window(): pl.pallas_call(functools.partial(window_kernel, n_gx=n_gx, n_gy=n_gy), in...  64.3 us
    pallas_call x1, Pallas kernels, collect(): pl.pallas_call(collect_kernel, in_specs=[pl.BlockSpec(memory_space=pltpu....  4.32 us

profile of v3, /device:TPU:0, one launch (start us, length us, event | category | flops | bytes accessed | tf_op | source)
XLA Modules:
  0.0 69.2 jit_solution(16165397626931163869)
XLA Ops:
  0.6 64.3 %window.1 = (f32[4,4096]{1,0:T(4,128)}, bf16[256,4096]{1,0:T(8,128)(2,1)}, bf16[128,16,256]{2,1,0:T(8,128)(2,1)}, s32[128]{0:T(128)}) custom-call(bf16[16,16,1024]{2,1,0:T(8,128)(2,1)} %latent.1, s32[1,1,128]{2,1,0:T(1,128)} %bitcast.3, bf16[64,1728]{1,0:T(8,128)(2,1)} %w1.1, bf16[64,1728]{1,0:T(8,128)(2,1)} %w2.1, bf16[320,256]{1,0:T(8,128)(2,1)} %w_in.1, ...), custom_call_target="tpu_custom_call" | custom-call | tf_op jit(solution)/shard_map/window/pallas_call | solution.py:347
  64.9 4.3 %collect.1 = (f32[16,16,1024]{2,1,0:T(8,128)}, f32[4,4096]{1,0:T(4,128)}, bf16[256,4096]{1,0:T(8,128)(2,1)}) custom-call(s32[128]{0:T(128)} %get-tuple-element.10.want_ref, bf16[128,16,256]{2,1,0:T(8,128)(2,1)} %get-tuple-element.11.back, f32[4,4096]{1,0:T(4,128)} %get-tuple-element.12.pred_in, bf16[256,4096]{1,0:T(8,128)(2,1)} %get-tuple-element.13.grads_in), custom_call_target="tpu_custom_call" | custom-call | tf_op jit(solution)/shard_map/collect/pallas_call | solution.py:415

commit v4 on v3

--- a/solution.py
+++ b/solution.py
@@ -10,13 +10,11 @@
 
 def gelu_pair(x):
     k = 0.7978845608028654
-    c = 0.044715
+    c = 0.044715 * k
     x2 = x * x
-    t = jnp.tanh(k * x * (1.0 + c * x2))
-    half = 0.5 * (1.0 + t)
-    value = x * half
-    slope = half + 0.5 * x * (1.0 - t * t) * (k * (1.0 + 3.0 * c * x2))
-    return value, slope
+    share = 0.5 * jnp.tanh(x * (k + c * x2)) + 0.5
+    slope = share * (1.0 + (1.0 - share) * (x * (2.0 * k + 6.0 * c * x2)))
+    return x * share, slope
 
 
 def gelu(x):
@@ -115,7 +113,9 @@
 
 MESH = pl.DeviceIdType.MESH
 PB = 1024
-CHUNKS = 8
+CHUNKS = 4
+SPAN = 1024
+STRIP = 16
 GROUPS = ((0, 32), (32, 64), (64, 96), (96, 128))
 
 
@@ -138,14 +138,6 @@
         index = lax.rem(me + k, count)
         return (index // n_gy, lax.rem(index, n_gy))
 
-    loads = [pltpu.make_async_copy(a, b, load_sem.at[i]) for i, (a, b) in enumerate([
-        (latent, latent_v), (w1, w1_v), (w2, w2_v), (w_in, w_in_v), (w_out, w_out_v), (cot, cot_v), (feat, feat_v),
-        (anchor, anchor_v), (frac, frac_v)])]
-    for load in loads:
-        load.start()
-    own_touch = pltpu.make_async_copy(touch.at[0], table_v.at[me], touch_own)
-    own_touch.start()
-
     along_y = [(gx, lax.rem(gy + j, n_gy)) for j in range(1, n_gy)]
     along_x = [(lax.rem(gx + i, n_gx), gy) for i in range(1, n_gx)]
     low_x, high_x = lax.rem(gx + n_gx - 1, n_gx), lax.rem(gx + 1, n_gx)
@@ -155,6 +147,14 @@
     greeted = diagonal + along_x + along_y
     for device in greeted:
         pl.semaphore_signal(barrier, inc=1, device_id=device, device_id_type=MESH)
+
+    loads = [pltpu.make_async_copy(a, b, load_sem.at[i]) for i, (a, b) in enumerate([
+        (latent, latent_v), (w1, w1_v), (w2, w2_v), (w_in, w_in_v), (w_out, w_out_v), (cot, cot_v), (feat, feat_v),
+        (anchor, anchor_v), (frac, frac_v)])]
+    for load in loads:
+        load.start()
+    own_touch = pltpu.make_async_copy(touch.at[0], table_v.at[me], touch_own)
+    own_touch.start()
 
     loads[0].wait()
     for c, y in enumerate((0, 1, 14, 15)):
@@ -181,26 +181,10 @@
         pltpu.make_async_remote_copy(src_ref=touch.at[0], dst_ref=table_v.at[me], send_sem=touch_send.at[0], recv_sem=touch_recv.at[0],
                                      device_id=device, device_id_type=MESH).start()
 
-    for load in loads[1:7]:
+    for load in loads[1:3]:
         load.wait()
-    wt[...] = w_in_v[...].T
-    wide = w_out_v[...].astype(f32).T
-    wo[...] = jnp.concatenate([wide, wide, wide, jnp.zeros_like(wide)], axis=1).astype(bf16)
     spread_weight(w1_v, band1)
     spread_weight(w2_v, band2)
-
-    def prepare(i, carry):
-        span = pl.ds(pl.multiple_of(i * PB, PB), PB)
-        state[:, span] = jnp.dot(wt[:, 64:], feat_v[:, span], preferred_element_type=f32)
-        given = cot_v[:, span]
-        high = given.astype(bf16).astype(f32)
-        rest = given - high
-        mid = rest.astype(bf16).astype(f32)
-        pieces = jnp.concatenate([high, mid, rest - mid, jnp.zeros_like(high)], axis=0).astype(bf16)
-        lift[:, span] = jnp.dot(wo[...], pieces, preferred_element_type=f32)
-        return carry
-
-    lax.fori_loop(0, blocks, prepare, 0)
 
     for copy in sides:
         copy.wait()
@@ -243,8 +227,11 @@
 
         lax.fori_loop(max(1, first), last, send_tile, 0)
     received[0] = outgoing[0]
-    for load in loads[7:]:
+    for load in loads[3:]:
         load.wait()
+    wt[...] = w_in_v[...].T
+    wide = w_out_v[...].astype(f32).T
+    wo[...] = jnp.concatenate([wide, wide, wide, jnp.zeros_like(wide)], axis=1).astype(bf16)
 
     def weigh(i, carry):
         span = pl.ds(pl.multiple_of(i * PB, PB), PB)
@@ -271,6 +258,19 @@
 
     lax.fori_loop(0, blocks, weigh, 0)
 
+    def prepare(i, carry):
+        span = pl.ds(pl.multiple_of(i * PB, PB), PB)
+        state[:, span] = jnp.dot(wt[:, 64:], feat_v[:, span], preferred_element_type=f32)
+        given = cot_v[:, span]
+        high = given.astype(bf16).astype(f32)
+        rest = given - high
+        mid = rest.astype(bf16).astype(f32)
+        pieces = jnp.concatenate([high, mid, rest - mid, jnp.zeros_like(high)], axis=0).astype(bf16)
+        lift[:, span] = jnp.dot(wo[...], pieces, preferred_element_type=f32)
+        return carry
+
+    lax.fori_loop(0, blocks, prepare, 0)
+
     for g, (first, last) in enumerate(GROUPS):
         arrived = max(1, first)
         wait_for(received.at[pl.ds(arrived, last - arrived)], tile_recv.at[g])
@@ -280,23 +280,21 @@
             value = jnp.dot(turned, near[first * 16 : last * 16, span], preferred_element_type=f32)
             mixed[:, span] = value if g == 0 else mixed[:, span] + value
 
-    def hidden(i, carry):
-        span = pl.ds(pl.multiple_of(i * PB, PB), PB)
+    for i in range(particles // SPAN):
+        span = slice(i * SPAN, (i + 1) * SPAN)
         wz = wz_v[:, span]
         sampled = mixed[0:64, span] * wz[0:1]
         for z in range(1, 4):
             sampled = sampled + mixed[z * 64 : z * 64 + 64, span] * wz[z : z + 1]
-        preact = state[:, span] + jnp.dot(wt[:, :64], sampled.astype(bf16), preferred_element_type=f32)
-        value, slope = gelu_pair(preact)
-        active[:, span] = value.astype(bf16)
-        grad = (lift[:, span] * slope).astype(bf16)
-        grad_pre[:, span] = grad
-        back = jnp.dot(w_in_v[0:64, :], grad, preferred_element_type=f32)
+        state[:, span] += jnp.dot(wt[:, :64], sampled.astype(bf16), preferred_element_type=f32)
+        for top in range(0, 256, STRIP):
+            strip = slice(top, top + STRIP)
+            value, slope = gelu_pair(state[strip, span])
+            active[strip, span] = value.astype(bf16)
+            grad_pre[strip, span] = (lift[strip, span] * slope).astype(bf16)
+        back = jnp.dot(w_in_v[0:64, :], grad_pre[:, span], preferred_element_type=f32)
         for z in range(4):
             spread[z * 64 : z * 64 + 64, span] = (back * wz[z : z + 1]).astype(bf16)
-        return carry
-
-    lax.fori_loop(0, blocks, hidden, 0)
 
     def scatter(q, carry):
         band = pl.ds(pl.multiple_of(q * part_slots * 16, part_slots * 16), part_slots * 16)
@@ -369,16 +367,19 @@
 
 
 LANES = 4
+PIECES = 4
 
 
 def collect_kernel(want_ref, back, pred_in, grads_in, grid_out, pred_out, grads_out, back_v, pred_v, grads_v, grid_v, *rest):
     sums, load_sem, store_sem = rest[:LANES], rest[LANES], rest[LANES + 1]
-    loads = [pltpu.make_async_copy(a, b, load_sem.at[i]) for i, (a, b) in enumerate([(back, back_v), (grads_in, grads_v), (pred_in, pred_v)])]
-    for load in loads:
+    size = back_v.shape[0] // PIECES
+    pieces = [pltpu.make_async_copy(back.at[pl.ds(i * size, size)], back_v.at[pl.ds(i * size, size)], load_sem.at[i]) for i in range(PIECES)]
+    grads_load = pltpu.make_async_copy(grads_in, grads_v, load_sem.at[PIECES])
+    pred_load = pltpu.make_async_copy(pred_in, pred_v, load_sem.at[PIECES + 1])
+    for load in [grads_load, pred_load] + pieces:
         load.start()
     for sum_ref in sums:
         sum_ref[...] = jnp.zeros_like(sum_ref)
-    loads[0].wait()
 
     def add(j, carry):
         for lane, sum_ref in enumerate(sums):
@@ -387,12 +388,15 @@
             sum_ref[jnp.where(wanted >= 0, wanted, 64)] += back_v[k].astype(jnp.float32)
         return carry
 
-    lax.fori_loop(0, back_v.shape[0] // LANES, add, 0, unroll=4)
-    loads[1].wait()
-    loads[2].wait()
-    stores = [pltpu.make_async_copy(a, b, store_sem.at[i]) for i, (a, b) in enumerate([(grads_v, grads_out), (pred_v, pred_out), (grid_v, grid_out)])]
-    stores[0].start()
-    stores[1].start()
+    grads_load.wait()
+    pred_load.wait()
+    stores = [pltpu.make_async_copy(grads_v, grads_out, store_sem.at[4]), pltpu.make_async_copy(pred_v, pred_out, store_sem.at[5])]
+    for store in stores:
+        store.start()
+    steps = size // LANES
+    for i in range(PIECES):
+        pieces[i].wait()
+        lax.fori_loop(i * steps, (i + 1) * steps, add, 0, unroll=4)
     for tx in range(4):
         for ty in range(4):
             for tz in range(4):
@@ -402,7 +406,9 @@
                     tile = tile + sum_ref[t]
                 for i in range(4):
                     grid_v[tx * 4 + i, ty * 4 : ty * 4 + 4, tz * 256 : tz * 256 + 256] = tile[i * 4 : i * 4 + 4]
-    stores[2].start()
+        store = pltpu.make_async_copy(grid_v.at[pl.ds(tx * 4, 4)], grid_out.at[pl.ds(tx * 4, 4)], store_sem.at[tx])
+        store.start()
+        stores.append(store)
     for store in stores:
         store.wait()
 
@@ -418,7 +424,7 @@
         out_specs=[hbm, hbm, hbm],
         out_shape=[grid, shaped(predicted.shape, predicted.dtype), shaped(grads.shape, grads.dtype)],
         scratch_shapes=[vmem(back), vmem(predicted), vmem(grads), vmem(grid)] + [pltpu.VMEM((65, 16, 256), jnp.float32)] * LANES
-        + [pltpu.SemaphoreType.DMA((3,)), pltpu.SemaphoreType.DMA((3,))],
+        + [pltpu.SemaphoreType.DMA((PIECES + 2,)), pltpu.SemaphoreType.DMA((6,))],
         compiler_params=pltpu.CompilerParams(vmem_limit_bytes=62 << 20),
         name="collect",
     )(want, back, predicted, grads)

time: 69.3 us -> 68.1 us (0.983)
  Pallas kernels: 68.6 us -> 67.2 us
    pallas_call x1, Pallas kernels: 64.3 us -> 63.2 us  [window(): pl.pallas_call(functools.partial(window_kernel, n_gx=n_gx, n_gy=n_gy), in...]
where the time goes in v4:
time: 68.1 us; the launch traced here: 68 us
  Pallas kernels  67.2 us (99%)
  between operations  0.8 us (1%)
    pallas_call x1, Pallas kernels, window(): pl.pallas_call(functools.partial(window_kernel, n_gx=n_gx, n_gy=n_gy), in...  63.2 us
    pallas_call x1, Pallas kernels, collect(): pl.pallas_call(collect_kernel, in_specs=[pl.BlockSpec(memory_space=pltpu....  4.03 us

profile of v4, /device:TPU:0, one launch (start us, length us, event | category | flops | bytes accessed | tf_op | source)
XLA Modules:
  0.0 68.0 jit_solution(7299277309592491241)
XLA Ops:
  0.6 63.2 %window.1 = (f32[4,4096]{1,0:T(4,128)}, bf16[256,4096]{1,0:T(8,128)(2,1)}, bf16[128,16,256]{2,1,0:T(8,128)(2,1)}, s32[128]{0:T(128)}) custom-call(bf16[16,16,1024]{2,1,0:T(8,128)(2,1)} %latent.1, s32[1,1,128]{2,1,0:T(1,128)} %bitcast.3, bf16[64,1728]{1,0:T(8,128)(2,1)} %w1.1, bf16[64,1728]{1,0:T(8,128)(2,1)} %w2.1, bf16[320,256]{1,0:T(8,128)(2,1)} %w_in.1, ...), custom_call_target="tpu_custom_call" | custom-call | tf_op jit(solution)/shard_map/window/pallas_call | solution.py:345
  63.8 4.0 %collect.1 = (f32[16,16,1024]{2,1,0:T(8,128)}, f32[4,4096]{1,0:T(4,128)}, bf16[256,4096]{1,0:T(8,128)(2,1)}) custom-call(s32[128]{0:T(128)} %get-tuple-element.10.want_ref, bf16[128,16,256]{2,1,0:T(8,128)(2,1)} %get-tuple-element.11.back, f32[4,4096]{1,0:T(4,128)} %get-tuple-element.12.pred_in, bf16[256,4096]{1,0:T(8,128)(2,1)} %get-tuple-element.13.grads_in), custom_call_target="tpu_custom_call" | custom-call | tf_op jit(solution)/shard_map/collect/pallas_call | solution.py:421

commit v5 on v4

--- a/solution.py
+++ b/solution.py
@@ -114,7 +114,7 @@
 MESH = pl.DeviceIdType.MESH
 PB = 1024
 CHUNKS = 4
-SPAN = 1024
+SPAN = 2048
 STRIP = 16
 GROUPS = ((0, 32), (32, 64), (64, 96), (96, 128))
 

time: 68.1 us -> 67.8 us (level)
  no operation moved by 1% of the time
where the time goes in v5:
time: 67.8 us; the launch traced here: 67.7 us
  Pallas kernels  66.9 us (99%)
  between operations  0.8 us (1%)
    pallas_call x1, Pallas kernels, window(): pl.pallas_call(functools.partial(window_kernel, n_gx=n_gx, n_gy=n_gy), in...  62.9 us
    pallas_call x1, Pallas kernels, collect(): pl.pallas_call(collect_kernel, in_specs=[pl.BlockSpec(memory_space=pltpu....  4.03 us

profile of v5, /device:TPU:0, one launch (start us, length us, event | category | flops | bytes accessed | tf_op | source)
XLA Modules:
  0.0 67.7 jit_solution(17551785911577483341)
XLA Ops:
  0.6 62.9 %window.1 = (f32[4,4096]{1,0:T(4,128)}, bf16[256,4096]{1,0:T(8,128)(2,1)}, bf16[128,16,256]{2,1,0:T(8,128)(2,1)}, s32[128]{0:T(128)}) custom-call(bf16[16,16,1024]{2,1,0:T(8,128)(2,1)} %latent.1, s32[1,1,128]{2,1,0:T(1,128)} %bitcast.3, bf16[64,1728]{1,0:T(8,128)(2,1)} %w1.1, bf16[64,1728]{1,0:T(8,128)(2,1)} %w2.1, bf16[320,256]{1,0:T(8,128)(2,1)} %w_in.1, ...), custom_call_target="tpu_custom_call" | custom-call | tf_op jit(solution)/shard_map/window/pallas_call | solution.py:345
  63.5 4.0 %collect.1 = (f32[16,16,1024]{2,1,0:T(8,128)}, f32[4,4096]{1,0:T(4,128)}, bf16[256,4096]{1,0:T(8,128)(2,1)}) custom-call(s32[128]{0:T(128)} %get-tuple-element.10.want_ref, bf16[128,16,256]{2,1,0:T(8,128)(2,1)} %get-tuple-element.11.back, f32[4,4096]{1,0:T(4,128)} %get-tuple-element.12.pred_in, bf16[256,4096]{1,0:T(8,128)(2,1)} %get-tuple-element.13.grads_in), custom_call_target="tpu_custom_call" | custom-call | tf_op jit(solution)/shard_map/collect/pallas_call | solution.py:421
